TPU v7x, 32 devices: a whole 2x2x4 slice. The times are simulated.
32 devices in a mesh: rep: 8 (over z, core), shard: 4 (over y, x).
Axes of the slice: x: 2, y: 2, z: 4, core: 2. Of those that a mesh axis runs over, the one named last changes fastest.
Arguments:
- hidden_in: bfloat16 [16384, 1536], P(('rep', 'shard')), may hold values from -6 to 6
- seg_ids: int32 [16384], P(('rep', 'shard')), may hold values from -1 to 1, as said below
- norm_gain: float32 [1536], replicated, may hold values from 0.1 to 1.9
- in_weight: bfloat16 [1536, 6448], P('shard'), may hold values from -0.15625 to 0.15625
- conv_weight: float32 [4, 3328], replicated, may hold values from -3 to 3
- conv_bias: float32 [3328], replicated, may hold values from -3 to 3
- dt_bias: float32 [48], replicated, may hold values from -6.5 to -3
- a_log: float32 [48], replicated, may hold values from 0 to 2.77
- skip_gain: float32 [48], replicated, may hold values from 0.5 to 2
- gate_gain: float32 [3072], replicated, may hold values from 0.1 to 1.9
- out_weight: bfloat16 [3072, 1536], P('shard'), may hold values from -0.109375 to 0.109375
- cotangent: bfloat16 [16384, 1536], P(('rep', 'shard')), may hold values from -6 to 6
Outputs:
- block_out: bfloat16 [16384, 1536], P(('rep', 'shard'))
- input_grad: float32 [16384, 1536], P(('rep', 'shard'))
- norm_gain_grad: float32 [1536], replicated
- in_weight_grad: float32 [1536, 6448], P('shard')
- conv_weight_grad: float32 [4, 3328], replicated
- conv_bias_grad: float32 [3328], replicated
- dt_bias_grad: float32 [48], replicated
- a_log_grad: float32 [48], replicated
- skip_gain_grad: float32 [48], replicated
- gate_gain_grad: float32 [3072], replicated
- out_weight_grad: float32 [3072, 1536], P('shard')
Inputs may be any that keep to these rules, and one draw needn't show every extreme that they name: `seg_ids`: within one device's 512 rows each id other than -1 marks one whole sequence of consecutive rows that begins at a multiple of 256; ids of sequences rise along the rows; no sequence spans two devices; some sequence has exactly 512 rows.
All inputs are finite; a program needn't handle non-finite values.
Results may differ from a plain program's by a relative error of at most 0.015.
Values may be sent and summed in bfloat16 or wider, within the bound.
No kernel may reach another device: no remote copies, remote signals or barrier semaphores. Data moves between devices by JAX's collectives and lax.ppermute only.
A program may use at most 256 MiB of HBM per device.

v0:
```python
from functools import partial

import jax
import jax.numpy as jnp
from jax import lax
from jax.sharding import PartitionSpec as P

STRETCH = 256


epsilon = 1e-05
HIGHEST = lax.Precision.HIGHEST


def rms_in(hidden, norm_gain):
    return (
        hidden * lax.rsqrt(jnp.mean(hidden * hidden, axis=-1, keepdims=True) + epsilon) * norm_gain
    )


def scan_block(head_count, carry_state, pieces):
    signal, writer, reader, step_size, log_decay, starts = pieces
    block_len = signal.shape[0]
    running = jnp.cumsum(log_decay, axis=0)
    local_index = jnp.cumsum(starts)
    carried = (local_index == 0).astype(jnp.float32)
    position = lax.broadcasted_iota(jnp.int32, (block_len, block_len), 0)
    column = lax.broadcasted_iota(jnp.int32, (block_len, block_len), 1)
    allowed = (local_index[:, None] == local_index[None, :]) & (column <= position)
    spread = running.T[:, :, None] - running.T[:, None, :]
    decays = jnp.exp(jnp.where(allowed[None], spread, -jnp.inf))
    scores = jnp.dot(reader, writer.T, precision=HIGHEST)
    mixing = decays * scores[None] * step_size.T[:, None, :]
    per_head = signal.reshape(block_len, head_count, -1)
    intra_out = jnp.einsum("hij,jhp->ihp", mixing, per_head, precision=HIGHEST)
    inter_out = (
        jnp.einsum("in,hnp->ihp", reader, carry_state, precision=HIGHEST)
        * (jnp.exp(running) * carried[:, None])[:, :, None]
    )
    reach_end = (local_index == local_index[-1]).astype(jnp.float32)
    end_weight = jnp.exp(running[-1][None, :] - running) * reach_end[:, None] * step_size
    next_state = carry_state * (jnp.exp(running[-1]) * carried[-1])[:, None, None] + jnp.einsum(
        "jn,jh,jhp->hnp", writer, end_weight, per_head, precision=HIGHEST
    )
    return (next_state, (intra_out + inter_out).reshape(block_len, -1))


def mixer(
    projected, seg_ids, conv_weight, conv_bias, dt_bias, a_log, skip_gain, gate_gain, block_len
):
    inner_dim = gate_gain.shape[0]
    head_count = dt_bias.shape[0]
    conv_width = conv_bias.shape[0]
    state_dim = (conv_width - inner_dim) // 2
    tap_count = conv_weight.shape[0]
    row_count = projected.shape[0]
    head_dim = inner_dim // head_count
    gate_cols = projected[:, :inner_dim]
    conv_in = projected[:, inner_dim : inner_dim + conv_width]
    dt_raw = projected[:, inner_dim + conv_width :]
    starts = jnp.concatenate(
        [jnp.ones((1,), jnp.int32), (seg_ids[1:] != seg_ids[:-1]).astype(jnp.int32)]
    )
    seq_index = jnp.cumsum(starts)
    summed = conv_bias + conv_weight[tap_count - 1] * conv_in
    for offset in range(1, tap_count):
        shifted = jnp.concatenate([jnp.zeros((offset, conv_width), jnp.float32), conv_in[:-offset]])
        earlier = jnp.concatenate([jnp.full((offset,), -1, jnp.int32), seq_index[:-offset]])
        usable = (earlier == seq_index).astype(jnp.float32)
        summed = summed + conv_weight[tap_count - 1 - offset] * shifted * usable[:, None]
    conv_out = jax.nn.silu(summed)
    signal = conv_out[:, :inner_dim]
    writer = conv_out[:, inner_dim : inner_dim + state_dim]
    reader = conv_out[:, inner_dim + state_dim :]
    step_size = jax.nn.softplus(dt_raw + dt_bias)
    log_decay = -jnp.exp(a_log) * step_size
    block_count = row_count // block_len

    def blocks(value):
        return value.reshape((block_count, block_len) + value.shape[1:])

    initial = jnp.zeros((head_count, state_dim, head_dim), jnp.float32)
    final_state, scanned = lax.scan(
        jax.checkpoint(partial(scan_block, head_count)),
        initial,
        (
            blocks(signal),
            blocks(writer),
            blocks(reader),
            blocks(step_size),
            blocks(log_decay),
            blocks(starts),
        ),
    )
    ssm_out = scanned.reshape(row_count, inner_dim) + (
        signal.reshape(row_count, head_count, head_dim) * skip_gain[:, None]
    ).reshape(row_count, inner_dim)
    gated = ssm_out * jax.nn.silu(gate_cols)
    live = (seg_ids >= 0).astype(jnp.float32)
    return (
        gated
        * lax.rsqrt(jnp.mean(gated * gated, axis=-1, keepdims=True) + epsilon)
        * gate_gain
        * live[:, None]
    )


def local(
    hidden_in,
    seg_ids,
    norm_gain,
    in_weight,
    conv_weight,
    conv_bias,
    dt_bias,
    a_log,
    skip_gain,
    gate_gain,
    out_weight,
    cotangent,
):
    hidden = hidden_in.astype(jnp.float32)
    normed_full, norm_back = jax.vjp(rms_in, hidden, norm_gain)
    normed = normed_full.astype(jnp.bfloat16)
    columns = normed
    projected = jnp.dot(
        columns,
        lax.all_gather(in_weight, "shard", axis=0, tiled=True),
        preferred_element_type=jnp.float32,
    )
    proj_low = lax.optimization_barrier(projected.astype(jnp.bfloat16)).astype(jnp.float32)

    def local_mixer(proj_vals, conv_w, conv_b, bias_dt, log_rate, skip_coef, gain_vals):
        return mixer(
            proj_vals, seg_ids, conv_w, conv_b, bias_dt, log_rate, skip_coef, gain_vals, STRETCH
        )

    mixer_full, mixer_back = jax.vjp(
        local_mixer, proj_low, conv_weight, conv_bias, dt_bias, a_log, skip_gain, gate_gain
    )
    mixer_out = mixer_full.astype(jnp.bfloat16)
    columns = mixer_out
    branch = jnp.dot(
        columns,
        lax.all_gather(out_weight, "shard", axis=0, tiled=True),
        preferred_element_type=jnp.float32,
    )
    block_out = (hidden + branch).astype(jnp.bfloat16)
    d_mixer = lax.dot_general(
        cotangent,
        lax.all_gather(out_weight, "shard", axis=0, tiled=True),
        (((1,), (1,)), ((), ())),
        preferred_element_type=jnp.float32,
    )
    grads = mixer_back(d_mixer)
    d_proj = grads[0].astype(jnp.bfloat16)
    d_normed = lax.dot_general(
        d_proj,
        lax.all_gather(in_weight, "shard", axis=0, tiled=True),
        (((1,), (1,)), ((), ())),
        preferred_element_type=jnp.float32,
    )
    d_hidden, d_gain = norm_back(d_normed)
    input_grad = cotangent.astype(jnp.float32) + d_hidden
    small = lax.psum(
        (d_gain, grads[1], grads[2], grads[3], grads[4], grads[5], grads[6]), ("rep", "shard")
    )
    columns = normed
    in_part = lax.psum_scatter(
        lax.dot_general(
            columns, d_proj, (((0,), (0,)), ((), ())), preferred_element_type=jnp.float32
        ).astype(jnp.bfloat16),
        "shard",
        scatter_dimension=0,
        tiled=True,
    )
    columns = mixer_out
    out_part = lax.psum_scatter(
        lax.dot_general(
            columns, cotangent, (((0,), (0,)), ((), ())), preferred_element_type=jnp.float32
        ).astype(jnp.bfloat16),
        "shard",
        scatter_dimension=0,
        tiled=True,
    )
    in_grad, out_grad = (
        lax.psum(in_part, "rep").astype(jnp.float32),
        lax.psum(out_part, "rep").astype(jnp.float32),
    )
    return (
        block_out,
        input_grad,
        small[0],
        in_grad,
        small[1],
        small[2],
        small[3],
        small[4],
        small[5],
        small[6],
        out_grad,
    )


def solution(mesh):
    placed = (
        P(("rep", "shard"), None),
        P(("rep", "shard")),
        P(),
        P("shard", None),
        P(),
        P(),
        P(),
        P(),
        P(),
        P(),
        P("shard", None),
        P(("rep", "shard"), None),
    )
    return jax.shard_map(
        local,
        mesh=mesh,
        in_specs=placed,
        out_specs=(
            P(("rep", "shard"), None),
            P(("rep", "shard"), None),
            P(),
            P("shard", None),
            P(),
            P(),
            P(),
            P(),
            P(),
            P(),
            P("shard", None),
        ),
        check_vma=False,
    )
```

profile of v0, /device:TPU:8, one launch (start us, length us, event | category | flops | bytes accessed | tf_op | source)
XLA Modules:
  0.0 1652.6 jit_solution(444927456024991647)
XLA Ops:
  11.0 183.4 %all-gather.3.cloned.1.call-done = bf16[1536,6448]{0,1:T(8,128)(2,1)} async-done(((bf16[384,6448]{0,1:T(8,128)(2,1)}), bf16[1536,6448]{0,1:T(8,128)(2,1)}) %all-gather.3.cloned.1.call-update) | async-done | bytes 19808272 | tf_op jit(solution)/shard_map/all_gather | solution.py:128
  194.4 15.2 convolution_convert_fusion.2
  221.3 4.8 convert_element_type.105
  226.1 4.7 copy-done.1
  231.7 16.0 fusion.84
  253.4 6.0 copy.298
  263.6 217.0 %while.41 = (s32[]{:T(128)}, f32[48,128,64]{1,2,0:T(8,128)}, f32[2,256,3072]{1,0,2:T(2,128)}, f32[2,48,128,64]{2,3,1,0:T(8,128)}, f32[2,256,48]{1,2,0:T(8,128)S(...) while((s32[]{:T(128)}, f32[48,128,64]{1,2,0:T(8,128)}, ...), condition=%wide.region_8.9_spmd.clone, body=%wide.region_3.8_spmd.clone.sunk | while | flops 4950488064 | bytes 46171732 | solution.py:83
  282.2 14.1 bitcast_add_fusion.13
  296.3 12.8 copy.326
  309.1 62.4 %dynamic_update_slice.78 = f32[2,256,3072]{1,0,2:T(2,128)} dynamic-update-slice(f32[2,256,3072]{1,0,2:T(2,128)} %get-tuple-element.1047, f32[1,256,3072]{1,0,2:T(1,128)S(1)} %copy.326, s32[]{:T(128)S(6)} %copy.355, s32[]{:T(128)} %constant.147.clone.1..sunk, s32[]{:T(128)} %constant.147.clone.1..sunk) | dynamic-update-slice | bytes 6291460 | tf_op jit(solution)/shard_map/jvp()/while/body/jit(dynamic_update_index_in_dim)/dynamic_update_slice | solution.py:83
  391.1 14.1 bitcast_add_fusion.13
  405.2 12.8 copy.326
  418.0 62.4 %dynamic_update_slice.78 = f32[2,256,3072]{1,0,2:T(2,128)} dynamic-update-slice(f32[2,256,3072]{1,0,2:T(2,128)} %get-tuple-element.1047, f32[1,256,3072]{1,0,2:T(1,128)S(1)} %copy.326, s32[]{:T(128)S(6)} %copy.355, s32[]{:T(128)} %constant.147.clone.1..sunk, s32[]{:T(128)} %constant.147.clone.1..sunk) | dynamic-update-slice | bytes 6291460 | tf_op jit(solution)/shard_map/jvp()/while/body/jit(dynamic_update_index_in_dim)/dynamic_update_slice | solution.py:83
  484.1 10.0 multiply_reduce_fusion.12
  494.1 13.0 multiply_reduce_fusion.9
  507.2 13.2 multiply_reduce_fusion.10
  520.4 8.2 reshape.691
  535.5 420.0 %while.42 = (s32[]{:T(128)}, f32[48,128,64]{1,2,0:T(8,128)}, f32[2,256,3072]{1,0,2:T(2,128)}, f32[2,256,128]{2,1,0:T(8,128)}, f32[2,256,128]{2,1,0:T(8,128)}, /*...) while((s32[]{:T(128)}, f32[48,128,64]{1,2,0:T(8,128)}, ...), condition=%wide.region_25.26_spmd.clone, body=%wide.region_11.25_spmd.clone.sunk | while | flops 11239769088 | bytes 157081408 | solution.py:83
  588.0 21.4 %fusion.211 = (f32[48,256]{1,0:T(8,128)}, f32[48,256]{1,0:T(8,128)}, f32[48,256]{1,0:T(8,128)}, f32[256,256]{1,0:T(8,128)}) fusion(f32[48,256]{1,0:T(8,128)} %copy.332, f32[256,256]{1,0:T(8,128)S(1)} %fusion.209, f32[48,256]{1,0:T(8,128)} %copy_bitcast_fusion.17, pred[256,256]{1,0:T(8,128)(4,1)} %fusion.210, f32[48,64,256]{2,1,0:T(8,128)S(1)} %bitcast.393, ...), kind=kOutput, calls=%fused_computation.62.clone.1 | convolution fusion | flops 2456711168 | bytes 7127040 | tf_op jit(solution)/shard_map/transpose(jvp())/while/body/eval_jaxpr/checkpoint/hij,jhp->ihp/dot_general | solution.py:35
  621.0 7.2 multiply_reduce_fusion.19
  636.2 6.5 fusion.216
  645.7 7.4 fusion.214
  653.1 12.7 bitcast_add_fusion.16
  670.3 12.7 copy.340
  689.4 62.4 %dynamic_update_slice.82 = f32[2,256,3072]{1,0,2:T(2,128)} dynamic-update-slice(f32[2,256,3072]{1,0,2:T(2,128)} %get-tuple-element.1091, f32[1,256,3072]{1,0,2:T(1,128)S(1)} %copy.340, s32[]{:T(128)S(6)} %sub.250, s32[]{:T(128)} %constant.147.clone.1..sunk.1, s32[]{:T(128)} %constant.147.clone.1..sunk.1) | dynamic-update-slice | bytes 6291460 | tf_op jit(solution)/shard_map/transpose(jvp())/while/body/jit(dynamic_update_index_in_dim)/dynamic_update_slice | solution.py:83
  783.9 21.4 %fusion.211 = (f32[48,256]{1,0:T(8,128)}, f32[48,256]{1,0:T(8,128)}, f32[48,256]{1,0:T(8,128)}, f32[256,256]{1,0:T(8,128)}) fusion(f32[48,256]{1,0:T(8,128)} %copy.332, f32[256,256]{1,0:T(8,128)S(1)} %fusion.209, f32[48,256]{1,0:T(8,128)} %copy_bitcast_fusion.17, pred[256,256]{1,0:T(8,128)(4,1)} %fusion.210, f32[48,64,256]{2,1,0:T(8,128)S(1)} %bitcast.393, ...), kind=kOutput, calls=%fused_computation.62.clone.1 | convolution fusion | flops 2456711168 | bytes 7127040 | tf_op jit(solution)/shard_map/transpose(jvp())/while/body/eval_jaxpr/checkpoint/hij,jhp->ihp/dot_general | solution.py:35
  817.0 7.2 multiply_reduce_fusion.19
  832.2 6.5 fusion.216
  841.6 7.4 fusion.214
  849.1 12.7 bitcast_add_fusion.16
  866.2 12.7 copy.340
  885.3 62.4 %dynamic_update_slice.82 = f32[2,256,3072]{1,0,2:T(2,128)} dynamic-update-slice(f32[2,256,3072]{1,0,2:T(2,128)} %get-tuple-element.1091, f32[1,256,3072]{1,0,2:T(1,128)S(1)} %copy.340, s32[]{:T(128)S(6)} %sub.250, s32[]{:T(128)} %constant.147.clone.1..sunk.1, s32[]{:T(128)} %constant.147.clone.1..sunk.1) | dynamic-update-slice | bytes 6291460 | tf_op jit(solution)/shard_map/transpose(jvp())/while/body/jit(dynamic_update_index_in_dim)/dynamic_update_slice | solution.py:83
  967.5 12.5 multiply_reduce_fusion.8
  980.0 10.0 multiply_reduce_fusion.7
  990.1 4.9 slice_multiply_fusion.1
  995.0 4.9 slice_multiply_fusion
  999.9 5.1 slice_multiply_fusion.2
  1006.7 13.9 fusion.110
  1020.6 18.8 %convolution_convert_fusion = bf16[1536,6448]{0,1:T(8,128)(2,1)} fusion(bf16[512,1536]{1,0:T(8,128)(2,1)S(1)} %copy-done.16, f32[1536]{0:T(1024)S(1)} %copy-done.53, f32[512]{0:T(512)S(1)} %copy-done.57, f32[512,3072]{0,1:T(8,128)} %get-tuple-element.798, f32[512,3328]{0,1:T(8,128)} %get-tuple-element.799, f32[512,48]{0,1:T(8,128)S(1)} %get-tuple-element.769), kind=kOutput, calls=%fused_computation.132 | convolution fusion | flops 10164781056 | bytes 34594816 | tf_op jit(solution)/shard_map/dot_general | solution.py:170
  1039.3 24.6 %copy.227 = bf16[1536,6448]{1,0:T(8,128)(2,1)} copy(bf16[1536,6448]{0,1:T(8,128)(2,1)} %convolution_convert_fusion) | data formatting | bytes 39616512
  1065.4 10.6 convolution_convert_fusion.1
  1076.0 169.1 %reduce-scatter.7.cloned.1.call-done = bf16[384,6448]{1,0:T(8,128)(2,1)} async-done(((bf16[1536,6448]{1,0:T(8,128)(2,1)}), bf16[384,6448]{1,0:T(8,128)(2,1)}) %reduce-scatter.7.cloned.1.call-update) | async-done | bytes 4952080
  1245.2 7.6 copy.228
  1252.8 90.9 %reduce-scatter.5.cloned.1.call-done = bf16[768,1536]{1,0:T(8,128)(2,1)} async-done(((bf16[3072,1536]{1,0:T(8,128)(2,1)}), bf16[768,1536]{1,0:T(8,128)(2,1)}) %reduce-scatter.5.cloned.1.call-update) | async-done | bytes 2359312 | tf_op jit(solution)/shard_map/reduce_scatter | solution.py:178
  1345.0 22.5 %fusion.91 = (f32[1536]{0:T(1024)}, f32[512]{0:T(512)S(1)}, f32[512,1536]{1,0:T(8,128)}) fusion(bf16[512,1536]{1,0:T(8,128)(2,1)S(1)} %copy-done.16, f32[512]{0:T(512)S(1)} %copy-done.57, f32[1536]{0:T(1024)S(1)} %copy-done.53, bf16[1536,6448]{0,1:T(8,128)(2,1)} %all-gather.3.cloned.1.call-done, f32[512,3072]{0,1:T(8,128)} %get-tuple-element.798, ...), kind=kOutput, calls=%fused_computation.176 | convolution fusion | flops 10157234176 | bytes 37748736 | tf_op jit(solution)/shard_map/dot_general | solution.py:157
  1368.3 12.3 fusion.96
  1383.1 118.4 %all-reduce.27.cloned.1.call-done = (bf16[384,6448]{0,1:T(8,128)(2,1)}, bf16[768,1536]{1,0:T(8,128)(2,1)}) async-done(((bf16[384,6448]{0,1:T(8,128)(2,1)}, bf16[768,1536]{1,0:T(8,128)(2,1)}), (bf16[384,6448]{0,1:T(8,128)(2,1)}, bf16[768,1536]{1,0:T(8,128)(2,1)})) %all-reduce.27.cloned.1.call-update) | async-done | bytes 7311376 | tf_op jit(solution)/shard_map/psum | solution.py:187
  1510.7 125.9 %all-reduce.25.cloned.1.call-done = (f32[1536]{0:T(1024)}, f32[4,3328]{1,0:T(4,128)}, f32[3328]{0:T(1024)}, f32[48]{0:T(128)}, f32[48]{0:T(128)}, /*index=5*/f32[48]{0:T(128)}, f32[3072]{0:T(1024)}) async-done(((f32[1536]{0:T(1024)}, f32[4,3328]{1,0:T(4,128)}, f32[3328]{0:T(1024)}, f32[48]{0:T(128)}, f32[48]{0:T(128)}, /*index=5*/f32[48]{0:T(128)}, f32[3072]{0:T(1024)}), (f32[1536]{0:T(1024)}, ...) | async-done | bytes 85584 | tf_op jit(solution)/shard_map/psum | solution.py:165
  (428 shorter events, 241.1 us)
Async XLA Ops:
  7.2 187.2 %copy-start.52 = (f32[1536]{0:T(1024)S(1)}, f32[1536]{0:T(1024)}, u32[]{:S(2)}) copy-start(f32[1536]{0:T(1024)} %param.18) | copy-start | bytes 18436
  7.2 187.2 %all-gather.3.cloned.1.call-start = ((), (), s32[]{:S(2)}) async-start(), calls=%async_computation.2 | async-start | bytes 24760320 | tf_op jit(solution)/shard_map/all_gather | solution.py:128
  8.0 486.1 %all-gather.5.cloned.1.call-start = ((), (), s32[]{:S(2)}) async-start(), calls=%async_computation.3 | async-start | bytes 11796480 | tf_op jit(solution)/shard_map/all_gather | solution.py:145
  8.7 1236.5 %reduce-scatter.7.cloned.1.call-start = ((), (), s32[]{:S(2)}) async-start(), calls=%async_computation.5 | async-start | bytes 25067520
  8.9 498.3 %copy-start.54 = (f32[512]{0:T(512)}, f32[512]{0:T(512)S(1)}, u32[]{:S(2)}) copy-start(f32[512]{0:T(512)S(1)} %compare_convert_fusion.4) | copy-start | bytes 6148
  8.9 217.2 %copy-start.62 = (f32[48]{0:T(128)}, f32[48]{0:T(128)S(1)}, u32[]{:S(2)}) copy-start(f32[48]{0:T(128)S(1)} %exponential_negate_fusion) | copy-start | bytes 580
  9.3 200.3 %copy-start.56 = (f32[512]{0:T(512)}, f32[512]{0:T(512)S(1)}, u32[]{:S(2)}) copy-start(f32[512]{0:T(512)S(1)} %fusion.106) | copy-start | bytes 6148
  10.8 496.4 %copy-start.27 = (f32[3072]{0:T(1024)}, f32[3072]{0:T(1024)S(1)}, u32[]{:S(2)}) copy-start(f32[3072]{0:T(1024)S(1)} %mul.764) | copy-start | bytes 36868
  10.9 220.8 %copy-start.29 = (f32[3328]{0:T(1024)}, f32[3328]{0:T(1024)S(1)}, u32[]{:S(2)}) copy-start(f32[3328]{0:T(1024)S(1)} %get-tuple-element.697) | copy-start | bytes 39940
  10.9 220.8 %copy-start.31 = (f32[3328]{0:T(1024)}, f32[3328]{0:T(1024)S(1)}, u32[]{:S(2)}) copy-start(f32[3328]{0:T(1024)S(1)} %get-tuple-element.699) | copy-start | bytes 39940
  10.9 220.8 %copy-start.33 = (f32[3328]{0:T(1024)}, f32[3328]{0:T(1024)S(1)}, u32[]{:S(2)}) copy-start(f32[3328]{0:T(1024)S(1)} %get-tuple-element.698) | copy-start | bytes 39940
  10.9 220.8 %copy-start.35 = (f32[3328]{0:T(1024)}, f32[3328]{0:T(1024)S(1)}, u32[]{:S(2)}) copy-start(f32[3328]{0:T(1024)S(1)} %get-tuple-element.700) | copy-start | bytes 39940
  11.0 220.7 %copy-start.39 = (f32[512]{0:T(512)}, f32[512]{0:T(512)S(1)}, u32[]{:S(2)}) copy-start(f32[512]{0:T(512)S(1)} %get-tuple-element.806) | copy-start | bytes 6148
  11.0 220.7 %copy-start.44 = (f32[512]{0:T(512)}, f32[512]{0:T(512)S(1)}, u32[]{:S(2)}) copy-start(f32[512]{0:T(512)S(1)} %get-tuple-element.805) | copy-start | bytes 6148
  11.0 220.7 %copy-start.46 = (f32[512]{0:T(512)}, f32[512]{0:T(512)S(1)}, u32[]{:S(2)}) copy-start(f32[512]{0:T(512)S(1)} %get-tuple-element.807) | copy-start | bytes 6148
  231.0 16.8 %copy-start.25 = (f32[512,48]{0,1:T(8,128)}, f32[512,48]{0,1:T(8,128)S(1)}, u32[]{:S(2)}) copy-start(f32[512,48]{0,1:T(8,128)S(1)} %get-tuple-element.782) | copy-start | bytes 294916
  484.1 23.1 %slice-start.2 = ((s8[6815744]{0:T(1024)(128)(4,1)}), s8[2621440]{0:T(1024)(128)(4,1)S(1)}, s32[]{:S(2)}) async-start(s8[6815744]{0:T(1024)(128)(4,1)} %bitcast.409), calls=%async_computation.10 | async-start | bytes 5242880
  494.1 13.1 copy-start.58
  494.1 13.1 slice-start.3
  494.1 13.1 copy-start.6
  494.1 13.1 copy-start.9
  559.7 22.5 %copy-start.7 = (f32[1,256,48]{2,1,0:T(8,128)}, f32[1,256,48]{2,1,0:T(8,128)S(1)}, u32[]{:S(2)}) copy-start(f32[1,256,48]{2,1,0:T(8,128)S(1)} %copy.331) | copy-start | bytes 147460 | tf_op jit(solution)/shard_map/transpose(jvp())/while
  587.9 21.4 %copy-start.14 = (f32[256,256]{1,0:T(8,128)}, f32[256,256]{1,0:T(8,128)S(1)}, u32[]{:S(2)}) copy-start(f32[256,256]{1,0:T(8,128)S(1)} %fusion.209) | copy-start | bytes 786436 | tf_op jit(solution)/shard_map/transpose(jvp())/while
  653.1 13.4 copy-start
  653.1 13.4 copy-start.13
  653.1 13.4 copy-start.49
  666.5 16.5 copy-start.12
  670.3 81.5 %copy-start.11 = (f32[2,256,128]{2,1,0:T(8,128)S(1)}, f32[2,256,128]{2,1,0:T(8,128)}, u32[]{:S(2)}) copy-start(f32[2,256,128]{2,1,0:T(8,128)} %copy-done.10) | copy-start | bytes 786436 | tf_op jit(solution)/shard_map/transpose(jvp())/while
  689.4 62.4 %copy-start.20 = (f32[2,256,48]{1,2,0:T(8,128)S(1)}, f32[2,256,48]{1,2,0:T(8,128)}, u32[]{:S(2)}) copy-start(f32[2,256,48]{1,2,0:T(8,128)} %copy-done.19) | copy-start | bytes 294916 | tf_op jit(solution)/shard_map/transpose(jvp())/while
  754.3 23.9 %copy-start.7 = (f32[1,256,48]{2,1,0:T(8,128)}, f32[1,256,48]{2,1,0:T(8,128)S(1)}, u32[]{:S(2)}) copy-start(f32[1,256,48]{2,1,0:T(8,128)S(1)} %copy.331) | copy-start | bytes 147460 | tf_op jit(solution)/shard_map/transpose(jvp())/while
  783.9 21.4 %copy-start.14 = (f32[256,256]{1,0:T(8,128)}, f32[256,256]{1,0:T(8,128)S(1)}, u32[]{:S(2)}) copy-start(f32[256,256]{1,0:T(8,128)S(1)} %fusion.209) | copy-start | bytes 786436 | tf_op jit(solution)/shard_map/transpose(jvp())/while
  849.0 12.8 copy-start.8
  849.0 12.8 copy-start.23
  849.0 13.4 copy-start
  849.1 13.4 copy-start.13
  849.1 13.4 copy-start.49
  862.4 16.5 copy-start.12
  866.2 81.5 %copy-start.11 = (f32[2,256,128]{2,1,0:T(8,128)S(1)}, f32[2,256,128]{2,1,0:T(8,128)}, u32[]{:S(2)}) copy-start(f32[2,256,128]{2,1,0:T(8,128)} %copy-done.10) | copy-start | bytes 786436 | tf_op jit(solution)/shard_map/transpose(jvp())/while
  885.3 62.4 %copy-start.20 = (f32[2,256,48]{1,2,0:T(8,128)S(1)}, f32[2,256,48]{1,2,0:T(8,128)}, u32[]{:S(2)}) copy-start(f32[2,256,48]{1,2,0:T(8,128)} %copy-done.19) | copy-start | bytes 294916 | tf_op jit(solution)/shard_map/transpose(jvp())/while
  1006.7 13.9 copy-start.16
  1006.7 13.9 copy-start.53
  1006.7 13.9 copy-start.57
  1064.0 279.6 %reduce-scatter.5.cloned.1.call-start = ((), (), s32[]{:S(2)}) async-start(), calls=%async_computation.4 | async-start | bytes 11796480 | tf_op jit(solution)/shard_map/reduce_scatter | solution.py:178
  1076.0 267.7 %copy-start.38 = (f32[3072]{0:T(1024)S(1)}, f32[3072]{0:T(1024)}, u32[]{:S(2)}) copy-start(f32[3072]{0:T(1024)} %get-tuple-element.766) | copy-start | bytes 36868
  1076.0 268.5 %copy-start.66 = (f32[48]{0:T(128)S(1)}, f32[48]{0:T(128)}, u32[]{:S(2)}) copy-start(f32[48]{0:T(128)} %param.23) | copy-start | bytes 580
  1076.0 425.5 %all-reduce.27.cloned.1.call-start = ((), (), s32[]{:S(2)}) async-start(), calls=%async_computation.7 | async-start | bytes 14622720 | tf_op jit(solution)/shard_map/psum | solution.py:187
  1343.7 292.9 %all-reduce.25.cloned.1.call-start = ((), (), s32[]{:S(2)}) async-start(), calls=%async_computation.6 | async-start | bytes 183296 | tf_op jit(solution)/shard_map/psum | solution.py:165
  1345.0 22.5 %copy-start.42 = (f32[512]{0:T(512)S(1)}, f32[512]{0:T(512)}, u32[]{:S(2)}) copy-start(f32[512]{0:T(512)} %copy-done.41) | copy-start | bytes 6148
  (52 other events, 296.8 us)
Sparse Core Ops, SparseCore 0:
  9.9 184.5 all-gather.2
  196.3 96.1 all-gather.4
  1064.1 181.0 reduce-scatter.6
  1248.7 94.8 reduce-scatter.4
  1345.9 155.4 all-reduce.26
  1508.9 127.6 all-reduce.24
where the time goes:
time: 1680 us; the launch traced here: 1650 us
  waiting for transfers between devices  689 us (41%)
  local copies, waits for them, and re-layouts  475 us (28%)
  matrix products  270 us (16%)
  other arithmetic  172 us (10%)
  loops' own time  30.9 us (2%)
    dynamic_update_slice x12, local copies, waits for them, and re-layouts, mixer(): lax.scan(jax.checkpoint(partial(scan_block, head_count)), initial, (block...  305 us
    all_gather x1, waiting for transfers between devices, local(): lax.all_gather(in_weight, 'shard', axis=0, tiled=True)  183 us
    unnamed x7, waiting for transfers between devices  171 us
    psum x1, waiting for transfers between devices, local(): lax.psum((d_gain, grads[1], grads[2], grads[3], grads[4], grads[5], grads...  126 us
    psum x1, waiting for transfers between devices, local(): lax.psum(in_part, 'rep').astype(jnp.float32)  118 us
    dot_general x6, matrix products, scan_block(): intra_out = jnp.einsum('hij,jhp->ihp', mixing, per_head, precision=HIGHEST)  96.4 us
    reduce_scatter x1, waiting for transfers between devices, local(): lax.psum_scatter(lax.dot_general(columns, cotangent, (((0,), (0,)), ((),...  90.9 us
    unnamed x134, local copies, waits for them, and re-layouts  57.5 us
  transfers between devices with their start and end apart: 6, of which 5 were waited for; matrix products, arithmetic and copies ran while one was open for 22% of the time, Pallas kernels for 0%

commit v1 on v0

v1 whole, which is shorter than its diff:
```python
from functools import partial

import jax
import jax.numpy as jnp
from jax import lax
from jax.experimental import pallas as pl
from jax.experimental.pallas import tpu as pltpu
from jax.sharding import Mesh, PartitionSpec as P

EPS = 1e-05
HIGHEST = lax.Precision.HIGHEST
F32 = jnp.float32
BF16 = jnp.bfloat16
LC = 128
HEADS_STEP = 8
HD = 64


def dot(a, b, dims=((1,), (0,)), precision=None):
    return lax.dot_general(
        a, b, (dims, ((), ())), preferred_element_type=F32, precision=precision
    )


NT = ((1,), (1,))


def sigmoid(v):
    return 0.5 * jnp.tanh(0.5 * v) + 0.5


def silu_and_slope(pre):
    s = sigmoid(pre)
    value = pre * s
    return value, s + value * (1.0 - s)


def split3(value, head_count):
    lane = lax.broadcasted_iota(jnp.int32, value.shape, 1)
    value = jnp.where(lane < head_count, value, 0.0)
    hi = value.astype(BF16)
    rest = value - hi.astype(F32)
    mid = rest.astype(BF16)
    low = (rest - mid.astype(F32)).astype(BF16)
    first = (hi.astype(F32) + pltpu.roll(mid.astype(F32), head_count, 1)).astype(BF16)
    return jnp.concatenate([first, low], axis=1)


def conv_forward(padded, row, lanes, weight, bias, taps, masks, rows):
    window = padded[pl.ds(row, rows + 8), lanes]
    pre = bias + weight[taps - 1 : taps, :] * window[8 : 8 + rows, :]
    for offset in range(1, taps):
        pre = pre + weight[taps - 1 - offset : taps - offset, :] * (
            window[8 - offset : 8 - offset + rows, :] * masks[offset - 1, pl.ds(row, rows), :]
        )
    return pre


def forward_kernel(
    head_count,
    x_in, bc_in, dt_in, wx, bx, wbc, bbc, dt_bias, a_log, skip, u_ref, allowed, edges, ex, exa,
    x_out, slope_out, y_out, s0_out, bc_out, bcs_out, stack_out, heads_out, at_out,
    padded, cb, bt, xdt, xw, state, d1, ea, ew, ax,
):
    rows = x_in.shape[0]
    chunks = rows // LC
    width = x_in.shape[1]
    taps = wx.shape[0]
    group = pl.program_id(0)

    @pl.when(group == 0)
    def _():
        padded[0:8, :] = jnp.zeros((8, width), F32)
        padded[8:, 0:256] = bc_in[...].astype(F32)
        tri = (
            lax.broadcasted_iota(jnp.int32, (LC, LC), 0)
            >= lax.broadcasted_iota(jnp.int32, (LC, LC), 1)
        ).astype(F32)
        for c in range(chunks):
            row = c * LC
            here = slice(row, row + LC)
            for t in range(2):
                lanes = slice(t * 128, t * 128 + 128)
                pre = conv_forward(
                    padded, row, lanes, wbc[:, lanes], bbc[:, lanes], taps, u_ref, LC
                )
                value, slope = silu_and_slope(pre)
                bc_out[here, lanes] = value.astype(BF16)
                bcs_out[here, lanes] = slope
            writer = bc_out[here, 0:128]
            reader = bc_out[here, 128:256]
            cb[here, :] = dot(reader, writer, NT) * allowed[here, :]
            bt[:, here] = writer.astype(F32).T.astype(BF16)
            v = dt_in[here, :].astype(F32) + dt_bias[...]
            step = jnp.maximum(v, 0.0) + jnp.log1p(jnp.exp(-jnp.abs(v)))
            decay = -jnp.exp(a_log[...]) * step
            a = dot(tri, decay, precision=HIGHEST)
            last = a[LC - 1 : LC, :]
            heads_out[0, here, :] = step
            heads_out[1, here, :] = decay
            at_out[c] = a.T
            stack_out[0, here, :] = split3(step, head_count)
            stack_out[1, here, :] = split3(jnp.exp(a) * edges[0, here, :], head_count)
            stack_out[2, here, :] = split3(jnp.exp(last - a) * edges[1, here, :], head_count)
            stack_out[3, here, :] = split3(a, head_count)

    padded[8:, :] = x_in[...].astype(F32)
    state[...] = jnp.zeros_like(state)

    def chunk(c, carry):
        row = pl.multiple_of(c * LC, LC)
        here = pl.ds(row, LC)
        d1[...] = dot(stack_out[0, here, :], ex[...])
        ea[...] = dot(stack_out[1, here, :], ex[...])
        ew[...] = dot(stack_out[2, here, :], ex[...])
        ax[...] = dot(stack_out[3, here, :], exa[...])
        s0 = state[...].astype(BF16)
        s0_out[pl.ds(c, 1), :, :] = s0[None]
        low = lax.broadcasted_iota(jnp.int32, (LC, 128), 1) < HD
        for p in range(width // 128):
            lanes = slice(p * 128, p * 128 + 128)
            pre = conv_forward(padded, row, lanes, wx[:, lanes], bx[:, lanes], taps, u_ref, LC)
            value, slope = silu_and_slope(pre)
            x_out[here, lanes] = value.astype(BF16)
            slope_out[here, lanes] = slope.astype(BF16)
            scaled = value * d1[:, lanes]
            xdt[:, lanes] = scaled.astype(BF16)
            xw[:, lanes] = (scaled * ew[:, lanes]).astype(BF16)
        reader = bc_out[here, 128:256]
        inter = dot(reader, s0)
        scores = cb[here, :]
        ats = at_out[c, pl.ds(pl.multiple_of(group * HEADS_STEP, 8), HEADS_STEP), :]
        for p in range(width // 128):
            lanes = slice(p * 128, p * 128 + 128)
            mixes = []
            for k in range(2):
                head = 2 * p + k
                arow = ats[head : head + 1, :]
                acol = ax[:, head * 128 : head * 128 + 128]
                mixes.append((jnp.exp(jnp.minimum(acol - arow, 0.0)) * scores).astype(BF16))
            pair = xdt[:, lanes]
            zero = jnp.zeros_like(pair)
            both = jnp.concatenate([jnp.where(low, pair, zero), jnp.where(low, zero, pair)], axis=0)
            y = dot(jnp.concatenate(mixes, axis=1), both)
            y = y + ea[:, lanes] * inter[:, lanes]
            y = y + skip[:, lanes] * x_out[here, lanes].astype(F32)
            y_out[here, lanes] = y.astype(BF16)
        state[...] = state[...] * ea[LC - 1 : LC, :] + dot(bt[:, here], xw[...])
        return carry

    lax.fori_loop(0, chunks, chunk, 0)


def run_forward(proj, inner, head_count, state_dim, conv_w, conv_b, dt_bias, a_log, skip, masks):
    rows = proj.shape[0]
    chunks = rows // LC
    width = HEADS_STEP * HD
    groups = inner // width
    taps = conv_w.shape[0]
    bc = 2 * state_dim
    const = lambda *index: (lambda g: index)
    full = lambda shape: pl.BlockSpec(shape, lambda g: (0,) * len(shape))
    col = lambda lead: pl.BlockSpec((lead, width), lambda g: (0, g))
    out_shape = (
        jax.ShapeDtypeStruct((rows, inner), BF16),
        jax.ShapeDtypeStruct((rows, inner), BF16),
        jax.ShapeDtypeStruct((rows, inner), BF16),
        jax.ShapeDtypeStruct((chunks, state_dim, inner), BF16),
        jax.ShapeDtypeStruct((rows, bc), BF16),
        jax.ShapeDtypeStruct((rows, bc), F32),
        jax.ShapeDtypeStruct((4, rows, 256), BF16),
        jax.ShapeDtypeStruct((2, rows, 128), F32),
        jax.ShapeDtypeStruct((chunks, 128, LC), F32),
    )
    return pl.pallas_call(
        partial(forward_kernel, head_count),
        grid=(groups,),
        in_specs=[
            col(rows),
            pl.BlockSpec((rows, bc), const(0, inner // bc)),
            pl.BlockSpec((rows, 128), const(0, (inner + bc) // 128)),
            col(taps),
            col(1),
            pl.BlockSpec((taps, bc), const(0, inner // bc)),
            pl.BlockSpec((1, bc), const(0, inner // bc)),
            full((1, 128)),
            full((1, 128)),
            col(1),
            full((taps - 1, rows, 128)),
            full((rows, 128)),
            full((2, rows, 128)),
            col(256),
            pl.BlockSpec((256, HEADS_STEP * 128), lambda g: (0, g)),
        ],
        out_specs=[
            col(rows),
            col(rows),
            col(rows),
            pl.BlockSpec((chunks, state_dim, width), lambda g: (0, 0, g)),
            full((rows, bc)),
            full((rows, bc)),
            full((4, rows, 256)),
            full((2, rows, 128)),
            full((chunks, 128, LC)),
        ],
        out_shape=out_shape,
        scratch_shapes=[
            pltpu.VMEM((rows + 8, width), F32),
            pltpu.VMEM((rows, 128), F32),
            pltpu.VMEM((state_dim, rows), BF16),
            pltpu.VMEM((LC, width), BF16),
            pltpu.VMEM((LC, width), BF16),
            pltpu.VMEM((state_dim, width), F32),
            pltpu.VMEM((LC, width), F32),
            pltpu.VMEM((LC, width), F32),
            pltpu.VMEM((LC, width), F32),
            pltpu.VMEM((LC, HEADS_STEP * 128), F32),
        ],
        cost_estimate=pl.CostEstimate(
            flops=20_000_000_000, bytes_accessed=20_000_000, transcendentals=0
        ),
        name="scan_forward",
    )(
        proj, proj, proj, conv_w, conv_b, conv_w, conv_b, dt_bias, a_log, skip,
        masks["u"], masks["allowed"], masks["edges"], masks["ex"], masks["exa"],
    )


def norm_kernel(y_ref, z_ref, dm_ref, gain, live_ref, mixer_out, d_y, d_z, gg_out, gated_s, slope_s):
    rows = y_ref.shape[0]
    inner = y_ref.shape[1]
    tiles = inner // 128
    live = live_ref[...]
    square = jnp.zeros((rows, 128), F32)
    mixed = jnp.zeros((rows, 128), F32)
    for t in range(tiles):
        lanes = slice(t * 128, t * 128 + 128)
        z = z_ref[:, lanes].astype(F32)
        gated = y_ref[:, lanes].astype(F32) * (z * sigmoid(z))
        gated_s[:, lanes] = gated
        square = square + gated * gated
        mixed = mixed + gated * (gain[:, lanes] * (dm_ref[:, lanes].astype(F32) * live))
    q = lax.rsqrt(jnp.sum(square, axis=1, keepdims=True) * (1.0 / inner) + EPS)
    r = jnp.sum(mixed, axis=1, keepdims=True) * (1.0 / inner)
    q = jnp.broadcast_to(q, (rows, 128))
    back = q * q * q * r
    keep = q * live

    @pl.when(pl.program_id(0) == 0)
    def _():
        gg_out[...] = jnp.zeros_like(gg_out)

    for t in range(tiles):
        lanes = slice(t * 128, t * 128 + 128)
        z = z_ref[:, lanes].astype(F32)
        s = sigmoid(z)
        gate = z * s
        slope = s + gate * (1.0 - s)
        gated = gated_s[:, lanes]
        scale = gain[:, lanes]
        mixer_out[:, lanes] = (gated * keep * scale).astype(BF16)
        m = dm_ref[:, lanes].astype(F32) * keep
        gg_out[:, lanes] += jnp.sum((m * gated).reshape(rows // 8, 8, 128), axis=0)
        d_gated = m * scale - gated * back
        d_y[:, lanes] = (d_gated * gate).astype(BF16)
        d_z[:, lanes] = (d_gated * y_ref[:, lanes].astype(F32) * slope).astype(BF16)


def run_norm(y, z, d_mixer, gain, live):
    rows, inner = y.shape
    block = 128
    spec = pl.BlockSpec((block, inner), lambda i: (i, 0))
    return pl.pallas_call(
        norm_kernel,
        grid=(rows // block,),
        in_specs=[
            spec, spec, spec,
            pl.BlockSpec((1, inner), lambda i: (0, 0)),
            pl.BlockSpec((block, 128), lambda i: (i, 0)),
        ],
        out_specs=[spec, spec, spec, pl.BlockSpec((8, inner), lambda i: (0, 0))],
        out_shape=(
            jax.ShapeDtypeStruct((rows, inner), BF16),
            jax.ShapeDtypeStruct((rows, inner), BF16),
            jax.ShapeDtypeStruct((rows, inner), BF16),
            jax.ShapeDtypeStruct((8, inner), F32),
        ),
        scratch_shapes=[pltpu.VMEM((block, inner), F32), pltpu.VMEM((block, 128), F32)],
        cost_estimate=pl.CostEstimate(
            flops=10_000_000_000, bytes_accessed=20_000_000, transcendentals=0
        ),
        name="gated_norm",
    )(y, z, d_mixer, gain, live)


def conv_backward(padded, row, lanes, x_ref, weight, taps, masks):
    x = x_ref[pl.ds(row, LC), lanes].astype(F32)
    window = padded[pl.ds(row, LC + 8), lanes]
    d0 = window[0:LC, :]
    fold = lambda v: jnp.sum(v.reshape(LC // 8, 8, 128), axis=0)
    result = weight[taps - 1 : taps, :] * d0
    sums = [fold(d0), fold(d0 * x)]
    for offset in range(1, taps):
        moved = window[offset : offset + LC, :] * masks[offset - 1, pl.ds(row, LC), :]
        result = result + weight[taps - 1 - offset : taps - offset, :] * moved
        sums.append(fold(moved * x))
    return result, sums


def backward_kernel(
    head_count,
    dy_ref, x_ref, slope_ref, x_in, bc_in, s0_ref, bc_ref, bcs_ref, stack, heads, at_ref, dt_in,
    wx, wbc, dt_bias, a_log, skip, um_ref, allowed_t, ex, exa, hs,
    dx_out, sums_out, dbc_out, sums_bc_out, ddt_out, small_out,
    padded, grad, cbt, dcbt, ct, d_writer, d_reader, prow, qcol, hsum, sgrow,
    d1, ea, ew, ax, inter, gb, dye, xdt, xw, sacc,
):
    rows = x_ref.shape[0]
    chunks = rows // LC
    width = x_ref.shape[1]
    taps = wx.shape[0]
    group = pl.program_id(0)
    tiles = width // 128

    @pl.when(group == 0)
    def _():
        padded[rows:, :] = jnp.zeros((8, width), F32)
        for c in range(chunks):
            here = slice(c * LC, c * LC + LC)
            writer = bc_ref[here, 0:128]
            reader = bc_ref[here, 128:256]
            cbt[here, :] = dot(writer, reader, NT) * allowed_t[here, :]
            ct[:, here] = reader.astype(F32).T.astype(BF16)
        for ref in (dcbt, d_writer, d_reader, prow, qcol, hsum, sgrow):
            ref[...] = jnp.zeros_like(ref)

    grad[...] = jnp.zeros_like(grad)
    low = lax.broadcasted_iota(jnp.int32, (LC, 128), 1) < HD
    lane = lax.broadcasted_iota(jnp.int32, (LC, 128), 1)

    def chunk(i, carry):
        c = chunks - 1 - i
        row = pl.multiple_of(c * LC, LC)
        here = pl.ds(row, LC)
        d1[...] = dot(stack[0, here, :], ex[...])
        ea[...] = dot(stack[1, here, :], ex[...])
        ew[...] = dot(stack[2, here, :], ex[...])
        ax[...] = dot(stack[3, here, :], exa[...])
        writer = bc_ref[here, 0:128]
        reader = bc_ref[here, 128:256]
        s0 = s0_ref[c]
        g = grad[...]
        g_low = g.astype(BF16)
        inter[...] = dot(reader, s0)
        gb[...] = dot(writer, g_low) * ew[...]
        fold = jnp.sum((s0.astype(F32) * g).reshape(s0.shape[0] // 8, 8, width), axis=0)
        fold = fold * ea[LC - 1 : LC, :]
        sgrow[pl.ds(pl.multiple_of(c * 8, 8), 8), :] += dot(fold.astype(BF16), hs[...])
        for p in range(tiles):
            lanes = slice(p * 128, p * 128 + 128)
            x = x_ref[here, lanes].astype(F32)
            dy = dy_ref[here, lanes].astype(F32)
            scaled = x * d1[:, lanes]
            xdt[:, lanes] = scaled.astype(BF16)
            xw[:, lanes] = (scaled * ew[:, lanes]).astype(BF16)
            weighted = dy * ea[:, lanes]
            dye[:, lanes] = weighted.astype(BF16)
            sacc[1, :, lanes] = (x * gb[:, lanes]).astype(BF16)
            sacc[2, :, lanes] = (weighted * inter[:, lanes]).astype(BF16)
            sacc[3, :, lanes] = (dy * x).astype(BF16)
        d_reader[here, :] += dot(dye[...], s0, NT)
        d_writer[here, :] += dot(xw[...], g_low, NT)
        scores = cbt[here, :]
        group_rows = pl.ds(pl.multiple_of(group * HEADS_STEP, 8), HEADS_STEP)
        ats = at_ref[c, group_rows, :]
        for p in range(tiles):
            lanes = slice(p * 128, p * 128 + 128)
            pair = dy_ref[here, lanes]
            src = xdt[:, lanes]
            zero = jnp.zeros_like(pair)
            src2 = jnp.concatenate([jnp.where(low, src, zero), jnp.where(low, zero, src)], axis=0)
            pair2 = jnp.concatenate([jnp.where(low, pair, zero), jnp.where(low, zero, pair)], axis=0)
            dm = dot(src2, pair, NT)
            mixes = []
            for k in range(2):
                head = 2 * p + k
                index = group * HEADS_STEP + head
                arow = ats[head : head + 1, :]
                acol = ax[:, head * 128 : head * 128 + 128]
                e = jnp.exp(jnp.minimum(arow - acol, 0.0))
                mixes.append((e * scores).astype(BF16))
                t = e * dm[k * LC : k * LC + LC, :]
                dcbt[here, :] += t
                qq = t * scores
                prow.at[c, group_rows, :][head : head + 1, :] = jnp.sum(qq, axis=0, keepdims=True)
                qcol[here, :] = jnp.where(
                    lane == index, jnp.sum(qq, axis=1, keepdims=True), qcol[here, :]
                )
            x = x_ref[here, lanes].astype(F32)
            dxdt = dot(jnp.concatenate(mixes, axis=1), pair2) + gb[:, lanes]
            sacc[0, :, lanes] = (x * dxdt).astype(BF16)
            dx = d1[:, lanes] * dxdt + skip[:, lanes] * pair.astype(F32)
            padded[here, lanes] = dx * slope_ref[here, lanes].astype(F32)
        for k in range(4):
            hsum[k, here, :] += dot(sacc[k], hs[...])
        grad[...] = g * ea[LC - 1 : LC, :] + dot(ct[:, here], dye[...])
        return carry

    lax.fori_loop(0, chunks, chunk, 0)

    sums_out[...] = jnp.zeros_like(sums_out)

    def conv_chunk(c, carry):
        row = pl.multiple_of(c * LC, LC)
        for p in range(tiles):
            lanes = slice(p * 128, p * 128 + 128)
            result, sums = conv_backward(padded, row, lanes, x_in, wx[:, lanes], taps, um_ref)
            dx_out[pl.ds(row, LC), lanes] = result.astype(BF16)
            for k in range(taps + 1):
                sums_out[k, :, lanes] += sums[k]
        return carry

    lax.fori_loop(0, chunks, conv_chunk, 0)

    @pl.when(group == pl.num_programs(0) - 1)
    def _():
        total_a = jnp.zeros((8, 128), F32)
        total_dt = jnp.zeros((8, 128), F32)
        total_skip = jnp.zeros((8, 128), F32)
        upper = (
            lax.broadcasted_iota(jnp.int32, (LC, LC), 0)
            <= lax.broadcasted_iota(jnp.int32, (LC, LC), 1)
        ).astype(F32)
        at_end = lax.broadcasted_iota(jnp.int32, (LC, 128), 0) == LC - 1
        fold = lambda v: jnp.sum(v.reshape(LC // 8, 8, 128), axis=0)
        sums_bc_out[...] = jnp.zeros_like(sums_bc_out)
        for c in range(chunks):
            here = slice(c * LC, c * LC + LC)
            writer = bc_ref[here, 0:128]
            reader = bc_ref[here, 128:256]
            d_scores = dcbt[here, :] * allowed_t[here, :]
            d_w = d_writer[here, :] + dot(d_scores.astype(BF16), reader)
            d_r = d_reader[here, :] + dot(d_scores.T.astype(BF16), writer)
            padded[here, 0:128] = d_w * bcs_ref[here, 0:128]
            padded[here, 128:256] = d_r * bcs_ref[here, 128:256]
            step = heads[0, here, :]
            decay = heads[1, here, :]
            q_state = step * hsum[1, here, :]
            da = prow[c].T - qcol[here, :] + hsum[2, here, :] - q_state
            ends = jnp.sum(q_state, axis=0, keepdims=True) + jnp.sum(
                sgrow[c * 8 : c * 8 + 8, :], axis=0, keepdims=True
            )
            da = da + jnp.where(at_end, ends, 0.0)
            d_decay = dot(upper, da, precision=HIGHEST)
            d_step = hsum[0, here, :] - jnp.exp(a_log[...]) * d_decay
            d_raw = d_step * sigmoid(dt_in[here, :].astype(F32) + dt_bias[...])
            d_raw = jnp.where(lane < head_count, d_raw, 0.0)
            ddt_out[here, :] = d_raw.astype(BF16)
            total_dt = total_dt + fold(d_raw)
            total_a = total_a + fold(d_decay * decay)
            total_skip = total_skip + fold(hsum[3, here, :])
        small_out[0] = total_dt
        small_out[1] = total_a
        small_out[2] = total_skip
        for c in range(chunks):
            row = c * LC
            for p in range(2):
                lanes = slice(p * 128, p * 128 + 128)
                result, sums = conv_backward(padded, row, lanes, bc_in, wbc[:, lanes], taps, um_ref)
                dbc_out[row : row + LC, lanes] = result.astype(BF16)
                for k in range(taps + 1):
                    sums_bc_out[k, :, lanes] += sums[k]


def run_backward(dy, saved, proj, head_count, state_dim, conv_w, dt_bias, a_log, skip, masks):
    x, slope, _, s0, bc_val, bc_slope, stack, heads, at = saved
    rows, inner = dy.shape
    chunks = rows // LC
    width = HEADS_STEP * HD
    groups = inner // width
    taps = conv_w.shape[0]
    bc = 2 * state_dim
    const = lambda *index: (lambda g: index)
    full = lambda shape: pl.BlockSpec(shape, lambda g: (0,) * len(shape))
    col = lambda lead: pl.BlockSpec((lead, width), lambda g: (0, g))
    return pl.pallas_call(
        partial(backward_kernel, head_count),
        grid=(groups,),
        in_specs=[
            col(rows),
            col(rows),
            col(rows),
            col(rows),
            pl.BlockSpec((rows, bc), const(0, inner // bc)),
            pl.BlockSpec((chunks, state_dim, width), lambda g: (0, 0, g)),
            full((rows, bc)),
            full((rows, bc)),
            full((4, rows, 256)),
            full((2, rows, 128)),
            full((chunks, 128, LC)),
            pl.BlockSpec((rows, 128), const(0, (inner + bc) // 128)),
            col(taps),
            pl.BlockSpec((taps, bc), const(0, inner // bc)),
            full((1, 128)),
            full((1, 128)),
            col(1),
            full((taps - 1, rows, 128)),
            full((rows, 128)),
            col(256),
            pl.BlockSpec((256, HEADS_STEP * 128), lambda g: (0, g)),
            pl.BlockSpec((width, 128), lambda g: (g, 0)),
        ],
        out_specs=[
            col(rows),
            pl.BlockSpec((taps + 1, 8, width), lambda g: (0, 0, g)),
            full((rows, bc)),
            full((taps + 1, 8, bc)),
            full((rows, 128)),
            full((3, 8, 128)),
        ],
        out_shape=(
            jax.ShapeDtypeStruct((rows, inner), BF16),
            jax.ShapeDtypeStruct((taps + 1, 8, inner), F32),
            jax.ShapeDtypeStruct((rows, bc), BF16),
            jax.ShapeDtypeStruct((taps + 1, 8, bc), F32),
            jax.ShapeDtypeStruct((rows, 128), BF16),
            jax.ShapeDtypeStruct((3, 8, 128), F32),
        ),
        scratch_shapes=[
            pltpu.VMEM((rows + 8, width), F32),
            pltpu.VMEM((state_dim, width), F32),
            pltpu.VMEM((rows, 128), F32),
            pltpu.VMEM((rows, 128), F32),
            pltpu.VMEM((state_dim, rows), BF16),
            pltpu.VMEM((rows, 128), F32),
            pltpu.VMEM((rows, 128), F32),
            pltpu.VMEM((chunks, 128, LC), F32),
            pltpu.VMEM((rows, 128), F32),
            pltpu.VMEM((4, rows, 128), F32),
            pltpu.VMEM((chunks * 8, 128), F32),
            pltpu.VMEM((LC, width), F32),
            pltpu.VMEM((LC, width), F32),
            pltpu.VMEM((LC, width), F32),
            pltpu.VMEM((LC, HEADS_STEP * 128), F32),
            pltpu.VMEM((LC, width), F32),
            pltpu.VMEM((LC, width), F32),
            pltpu.VMEM((LC, width), BF16),
            pltpu.VMEM((LC, width), BF16),
            pltpu.VMEM((LC, width), BF16),
            pltpu.VMEM((4, LC, width), BF16),
        ],
        cost_estimate=pl.CostEstimate(
            flops=40_000_000_000, bytes_accessed=20_000_000, transcendentals=0
        ),
        name="scan_backward",
    )(
        dy, x, slope, proj, proj, s0, bc_val, bc_slope, stack, heads, at, proj,
        conv_w, conv_w, dt_bias, a_log, skip, masks["um"], masks["allowed_t"],
        masks["ex"], masks["exa"], masks["hs"],
    )


def make_masks(seg_ids, taps, head_count, inner):
    rows = seg_ids.shape[0]
    chunks = rows // LC
    starts = jnp.concatenate(
        [jnp.ones((1,), jnp.int32), (seg_ids[1:] != seg_ids[:-1]).astype(jnp.int32)]
    )
    tri = lax.broadcasted_iota(jnp.int32, (rows, rows), 0) >= lax.broadcasted_iota(
        jnp.int32, (rows, rows), 1
    )
    seq = jnp.sum(jnp.where(tri, starts[None, :], 0), axis=1)
    wide = lambda v: jnp.broadcast_to(v.astype(F32)[:, None], (rows, 128))
    u, um = [], []
    for offset in range(1, taps):
        same = seq[offset:] == seq[:-offset]
        none = jnp.zeros((offset,), jnp.bool_)
        u.append(wide(jnp.concatenate([none, same])))
        um.append(wide(jnp.concatenate([same, none])))
    by_chunk = seq.reshape(chunks, LC)
    order = lax.broadcasted_iota(jnp.int32, (LC, LC), 0)
    other = lax.broadcasted_iota(jnp.int32, (LC, LC), 1)
    same = by_chunk[:, :, None] == by_chunk[:, None, :]
    allowed = (same & (other <= order)[None]).astype(F32).reshape(rows, LC)
    allowed_t = (same & (order <= other)[None]).astype(F32).reshape(rows, LC)
    before = jnp.concatenate([jnp.full((1,), -1, jnp.int32), by_chunk[:-1, -1]])
    carried = (by_chunk == before[:, None]).reshape(rows)
    reach = (by_chunk == by_chunk[:, -1:]).reshape(rows)
    head_of = lambda width, size: (
        lax.broadcasted_iota(jnp.int32, (256, width), 1) // size
    )
    slot = lax.broadcasted_iota(jnp.int32, (256, 1), 0)
    part = jnp.where(
        slot < head_count,
        slot,
        jnp.where(
            slot < 2 * head_count,
            slot - head_count,
            jnp.where((slot >= 128) & (slot < 128 + head_count), slot - 128, -1),
        ),
    )
    ex = (part == head_of(inner, HD)).astype(BF16)
    exa = (part == head_of(head_count * 128, 128)).astype(BF16)
    hs = (
        lax.broadcasted_iota(jnp.int32, (inner, 128), 0) // HD
        == lax.broadcasted_iota(jnp.int32, (inner, 128), 1)
    ).astype(BF16)
    return {
        "u": jnp.stack(u),
        "um": jnp.stack(um),
        "allowed": allowed,
        "allowed_t": allowed_t,
        "edges": jnp.stack([wide(carried), wide(reach)]),
        "ex": ex,
        "exa": exa,
        "hs": hs,
        "live": wide(seg_ids >= 0),
    }


def swap(value):
    return lax.ppermute(value, "core", [(0, 1), (1, 0)])


def all_sum(value, axes):
    for axis, size in axes:
        step = 1
        while step < size:
            value = value + lax.ppermute(value, axis, [(i, i ^ step) for i in range(size)])
            step *= 2
    return value


def local(
    sizes,
    hidden_in,
    seg_ids,
    norm_gain,
    in_weight,
    conv_weight,
    conv_bias,
    dt_bias,
    a_log,
    skip_gain,
    gate_gain,
    out_weight,
    cotangent,
):
    line_n, core_n, shard_n = sizes
    core = lax.axis_index("core")
    rows, width = hidden_in.shape
    inner = gate_gain.shape[0]
    heads = dt_bias.shape[0]
    taps, xbc = conv_weight.shape
    state_dim = (xbc - inner) // 2
    shard_rows = in_weight.shape[0]
    half = shard_rows // 2
    f_rest = in_weight.shape[1] - inner
    f_pad = -f_rest % 128

    def split_cols(value):
        parts = value.reshape(value.shape[0], shard_n, 2, half)
        mine = lax.dynamic_index_in_dim(parts, core, 2, keepdims=False)
        other = lax.dynamic_index_in_dim(parts, 1 - core, 2, keepdims=False)
        flat = (value.shape[0], shard_n * half)
        return mine.reshape(flat), other.reshape(flat)

    def by_core(mine, other):
        first = jnp.where(core == 0, mine, other)
        second = jnp.where(core == 0, other, mine)
        return first, second

    def join_cols(mine, other):
        shape = (mine.shape[0], shard_n, half)
        first, second = by_core(mine.reshape(shape), other.reshape(shape))
        return jnp.stack([first, second], axis=2).reshape(mine.shape[0], width)

    own_rows = lax.dynamic_slice_in_dim(in_weight, core * half, half, 0)
    w1_own = jnp.pad(own_rows[:, inner:], ((0, 0), (0, f_pad)))
    w1_m = lax.all_gather(w1_own, "shard", axis=0, tiled=True)
    w1_o = swap(w1_m)
    w0_m = lax.all_gather(own_rows[:, :inner], "shard", axis=0, tiled=True)
    w0_o = swap(w0_m)
    wo_own, _ = split_cols(out_weight)
    wo_m = lax.all_gather(wo_own, "shard", axis=0, tiled=True)
    wo_o = swap(wo_m)

    masks = make_masks(seg_ids, taps, heads, inner)
    pad_heads = lambda v: jnp.pad(v, (0, 128 - heads))[None]
    dt_bias_p, a_log_p = pad_heads(dt_bias), pad_heads(a_log)
    skip_wide = jnp.repeat(skip_gain, HD)[None]

    hid_m, hid_o = split_cols(hidden_in)
    cot_m, cot_o = split_cols(cotangent)
    gain_m, gain_o = split_cols(norm_gain[None])
    h_m, h_o = hid_m.astype(F32), hid_o.astype(F32)
    square = jnp.sum(h_m * h_m, axis=-1, keepdims=True) + jnp.sum(h_o * h_o, axis=-1, keepdims=True)
    r = lax.rsqrt(square * (1.0 / width) + EPS)
    n_m = (h_m * r * gain_m).astype(BF16)
    n_o = (h_o * r * gain_o).astype(BF16)

    proj1 = (dot(n_m, w1_m) + dot(n_o, w1_o)).astype(BF16)
    saved = run_forward(
        proj1, inner, heads, state_dim, conv_weight, conv_bias[None], dt_bias_p, a_log_p,
        skip_wide, masks,
    )
    gate = (dot(n_m, w0_m) + dot(n_o, w0_o)).astype(BF16)
    d_mixer = (dot(cot_m, wo_m, NT) + dot(cot_o, wo_o, NT)).astype(BF16)
    mixer_out, d_y, d_gate, gg = run_norm(saved[2], gate, d_mixer, gate_gain[None], masks["live"])

    tn = ((0,), (0,))

    def reduce_pair(lhs_m, lhs_o, rhs_m, rhs_o):
        sent = swap(dot(lhs_o, rhs_o, tn).astype(BF16))
        return (dot(lhs_m, rhs_m, tn) + sent.astype(F32)).astype(BF16)

    def reduce_rest(value):
        part = lax.psum_scatter(value, "shard", scatter_dimension=0, tiled=True)
        return lax.psum(part, "line")

    g0 = reduce_rest(reduce_pair(n_m, n_o, d_gate, d_gate))
    go = reduce_rest(reduce_pair(mixer_out, mixer_out, cot_m, cot_o))

    d_x, x_sums, d_bc, bc_sums, d_dt, small = run_backward(
        d_y, saved, proj1, heads, state_dim, conv_weight, dt_bias_p, a_log_p, skip_wide, masks
    )
    d_proj1 = jnp.concatenate([d_x, d_bc, d_dt], axis=1)
    g1 = reduce_rest(reduce_pair(n_m, n_o, d_proj1, d_proj1))

    branch_m, branch_o = dot(mixer_out, wo_m), dot(mixer_out, wo_o)
    block_out = join_cols((h_m + branch_m).astype(BF16), (h_o + branch_o).astype(BF16))

    dn_m = dot(d_gate, w0_m, NT) + dot(d_proj1, w1_m, NT)
    dn_o = dot(d_gate, w0_o, NT) + dot(d_proj1, w1_o, NT)
    ng = join_cols(
        jnp.sum(dn_m * h_m * r, axis=0, keepdims=True), jnp.sum(dn_o * h_o * r, axis=0, keepdims=True)
    )[0]
    gd_m, gd_o = gain_m * dn_m, gain_o * dn_o
    mean = (
        jnp.sum(h_m * gd_m, axis=-1, keepdims=True) + jnp.sum(h_o * gd_o, axis=-1, keepdims=True)
    ) * (1.0 / width)
    back = r * r * r * mean
    input_grad = join_cols(
        cot_m.astype(F32) + r * gd_m - h_m * back, cot_o.astype(F32) + r * gd_o - h_o * back
    )

    sums = jnp.concatenate([x_sums.sum(1), bc_sums.sum(1)], axis=1)
    per_head = small.sum(1)
    packed = jnp.concatenate([sums.reshape(-1), per_head.reshape(-1), gg.sum(0), ng])
    packed = jnp.pad(packed, (0, -packed.shape[0] % 1024)).reshape(-1, 128)
    packed = all_sum(packed, (("core", core_n), ("shard", shard_n), ("line", line_n))).reshape(-1)
    sums = packed[: (taps + 1) * xbc].reshape(taps + 1, xbc)
    at = (taps + 1) * xbc
    per_head = packed[at : at + 384].reshape(3, 128)[:, :heads]
    at += 384
    gate_gain_grad = packed[at : at + inner]
    norm_gain_grad = packed[at + inner : at + inner + width]

    g0_first, g0_second = by_core(g0, swap(g0))
    g1_first, g1_second = by_core(g1[:, :f_rest], swap(g1)[:, :f_rest])
    in_grad = jnp.concatenate(
        [
            jnp.concatenate([g0_first, g1_first], axis=1),
            jnp.concatenate([g0_second, g1_second], axis=1),
        ],
        axis=0,
    ).astype(F32)
    out_grad = join_cols(go, swap(go)).astype(F32)
    return (
        block_out,
        input_grad,
        norm_gain_grad,
        in_grad,
        sums[1:][::-1],
        sums[0],
        per_head[0],
        per_head[1],
        per_head[2],
        gate_gain_grad,
        out_grad,
    )


def solution(mesh):
    rep_n, shard_n = mesh.devices.shape
    sizes = (rep_n // 2, 2, shard_n)
    fine = Mesh(mesh.devices.reshape(sizes), ("line", "core", "shard"))
    tokens = ("line", "core", "shard")
    placed = (
        P(tokens, None),
        P(tokens),
        P(),
        P("shard", None),
        P(),
        P(),
        P(),
        P(),
        P(),
        P(),
        P("shard", None),
        P(tokens, None),
    )
    return jax.shard_map(
        partial(local, sizes),
        mesh=fine,
        in_specs=placed,
        out_specs=(
            P(tokens, None),
            P(tokens, None),
            P(),
            P("shard", None),
            P(),
            P(),
            P(),
            P(),
            P(),
            P(),
            P("shard", None),
        ),
        check_vma=False,
    )
```

time: 1680 us -> 697 us (0.41); the launches traced: 1650 us -> 690 us
  local copies, waits for them, and re-layouts: 475 us -> 81.9 us
  waiting for transfers between devices: 689 us -> 360 us
  matrix products: 270 us -> 91.8 us
  other arithmetic: 172 us -> 51.6 us
  Pallas kernels: 0 us -> 80.8 us
  loops' own time: 30.9 us -> 0 us
    dynamic_update_slice x12 -> x0, local copies, waits for them, and re-layouts: 305 us -> none  [mixer(): lax.scan(jax.checkpoint(partial(scan_block, head_count)), initial, (block...]
    unnamed x7, waiting for transfers between devices: 171 us -> 0.11 us
    dot_general x30 -> x18, matrix products: 256 us -> 91.8 us  [dot(): lax.dot_general(a, b, (dims, ((), ())), preferred_element_type=F32, preci...]
    psum x2 -> x1, waiting for transfers between devices: 244 us -> 112 us  [reduce_rest(): return lax.psum(part, 'line')]
    pallas_call x0 -> x3, Pallas kernels: none -> 80.8 us  [the longest x1 43.8 us: run_backward(): pl.pallas_call(partial(backward_kernel, head_count), grid=(groups,), in_s...]
    reduce_sum x14 -> x6, other arithmetic: 72.8 us -> 1.72 us  [the longest x2 1.19 us: local(): sums = jnp.concatenate([x_sums.sum(1), bc_sums.sum(1)], axis=1)]
    mul x14 -> x1, other arithmetic: 39.1 us -> 0.01 us  [local(): back = r * r * r * mean]
    all_gather x2 -> x3, waiting for transfers between devices: 183 us -> 150 us  [the longest x1 62.8 us: local(): w1_m = lax.all_gather(w1_own, 'shard', axis=0, tiled=True)]
  transfers between devices with their start and end apart: 6 -> 21, of which waited for: 5 -> 10; matrix products, arithmetic and copies ran while one was open for 22% -> 25% of each run, Pallas kernels for 0% -> 6%
where the time goes in v1:
time: 697 us; the launch traced here: 690 us
  waiting for transfers between devices  360 us (52%)
  matrix products  91.8 us (13%)
  local copies, waits for them, and re-layouts  81.9 us (12%)
  Pallas kernels  80.8 us (12%)
  other arithmetic  51.6 us (7%)
  between operations  15.2 us (2%)
  starting transfers between devices  8.67 us (1%)
    psum x1, waiting for transfers between devices, reduce_rest(): return lax.psum(part, 'line')  112 us
    dot_general x18, matrix products, dot(): lax.dot_general(a, b, (dims, ((), ())), preferred_element_type=F32, preci...  91.8 us
    reduce_scatter x3, waiting for transfers between devices, reduce_rest(): part = lax.psum_scatter(value, 'shard', scatter_dimension=0, tiled=True)  76.5 us
    all_gather x1, waiting for transfers between devices, local(): w1_m = lax.all_gather(w1_own, 'shard', axis=0, tiled=True)  62.8 us
    all_gather x1, waiting for transfers between devices, local(): wo_m = lax.all_gather(wo_own, 'shard', axis=0, tiled=True)  56.7 us
    pallas_call x1, Pallas kernels, run_backward(): pl.pallas_call(partial(backward_kernel, head_count), grid=(groups,), in_s...  43.8 us
    unnamed x99, local copies, waits for them, and re-layouts  35.1 us
    all_gather x1, waiting for transfers between devices, local(): w0_m = lax.all_gather(own_rows[:, :inner], 'shard', axis=0, tiled=True)  30.7 us
  transfers between devices with their start and end apart: 21, of which 10 were waited for; matrix products, arithmetic and copies ran while one was open for 25% of the time, Pallas kernels for 6%

profile of v1, /device:TPU:8, one launch (start us, length us, event | category | flops | bytes accessed | tf_op | source)
XLA Modules:
  0.0 690.3 jit_solution(13293743163046752687)
XLA Ops:
  7.2 2.4 constant_dynamic-slice_fusion.3
  11.2 2.8 copy.122
  15.2 2.8 dynamic-slice
  23.9 2.4 dynamic-slice_convert_fusion.1
  28.3 3.6 copy.120
  38.7 30.7 %all-gather.6.cloned.1.call-done = bf16[768,3072]{1,0:T(8,128)(2,1)} async-done(((bf16[192,3072]{1,0:T(8,128)(2,1)}), bf16[768,3072]{1,0:T(8,128)(2,1)}) %all-gather.6.cloned.1.call-update) | async-done | bytes 4718608 | tf_op jit(solution)/shard_map/all_gather | solution.py:682
  71.6 56.7 %all-gather.8.cloned.1.call-done = bf16[3072,768]{0,1:T(8,128)(2,1)} async-done(((bf16[768,768]{0,1:T(8,128)(2,1)}), bf16[3072,768]{0,1:T(8,128)(2,1)}) %all-gather.8.cloned.1.call-update) | async-done | bytes 4718608 | tf_op jit(solution)/shard_map/all_gather | solution.py:685
  129.8 62.8 %all-gather.4.cloned.1.call-done = bf16[768,3456]{1,0:T(8,128)(2,1)} async-done(((bf16[192,3456]{1,0:T(8,128)(2,1)}), bf16[768,3456]{1,0:T(8,128)(2,1)}) %all-gather.4.cloned.1.call-update) | async-done | bytes 5308432 | tf_op jit(solution)/shard_map/all_gather | solution.py:680
  192.6 2.4 fusion.exa
  195.0 4.6 fusion.21
  199.7 2.8 fusion.22
  202.5 3.0 fusion.20
  205.5 6.6 add_convert_fusion.5.z_ref
  212.1 6.6 add_convert_fusion.4.dm_ref
  218.8 7.3 %add_convert_fusion.3.x_in.bc_in.dt_in = bf16[512,3456]{1,0:T(8,128)(2,1)} fusion(f32[512,3456]{1,0:T(8,128)S(1)} %fusion.20, bf16[512,768]{1,0:T(8,128)(2,1)S(1)} %copy-done.18, bf16[768,3456]{1,0:T(8,128)(2,1)} %collective-permute-done), kind=kOutput, calls=%fused_computation.3 | convolution fusion | flops 2721447936 | bytes 16711680 | tf_op jit(solution)/shard_map/dot_general | solution.py:20
  226.0 25.0 %scan_forward.1 = (bf16[512,3072]{1,0:T(8,128)(2,1)}, bf16[512,3072]{1,0:T(8,128)(2,1)}, bf16[512,3072]{1,0:T(8,128)(2,1)}, bf16[4,128,3072]{2,1,0:T(8,128)(2,1)...) custom-call(bf16[512,3456]{1,0:T(8,128)(2,1)} %add_convert_fusion.3., ...), custom_call_target="tpu_custom_call" | custom-call | flops 20000000000 | bytes 20000000 | tf_op jit(solution)/shard_map/scan_forward/pallas_call | solution.py:175
  251.9 12.0 %gated_norm.1 = (bf16[512,3072]{1,0:T(8,128)(2,1)}, bf16[512,3072]{1,0:T(8,128)(2,1)}, bf16[512,3072]{1,0:T(8,128)(2,1)}, f32[8,3072]{1,0:T(8,128)}) custom-call(bf16[512,3072]{1,0:T(8,128)(2,1)} %get-tuple-element.30.y_ref, bf16[512,3072]{1,0:T(8,128)(2,1)} %add_convert_fusion.5.z_ref, bf16[512,3072]{1,0:T(8,128)(2,1)} %add_convert_fusion.4.dm_ref, ...), custom_call_target="tpu_custom_call" | custom-call | flops 10000000000 | bytes 20000000 | tf_op jit(solution)/shard_map/gated_norm/pallas_call | solution.py:273
  264.0 4.9 convolution_convert_fusion.2
  269.5 7.5 %collective-permute-done.8 = bf16[768,3072]{1,0:T(8,128)(2,1)S(1)} collective-permute-done((bf16[768,3072]{1,0:T(8,128)(2,1)S(1)}, bf16[768,3072]{1,0:T(8,128)(2,1)S(1)}, u32[]{:S(2)}, u32[]{:S(2)}) %collective-permute-start.8) | collective-permute-done | bytes 4718624 | tf_op jit(solution)/shard_map/ppermute | solution.py:622
  277.0 4.3 add_convert_fusion.2
  281.4 4.6 convolution_convert_fusion.1
  287.8 4.0 fusion.2.hs
  293.9 4.3 add_convert_fusion.1
  298.4 43.8 %scan_backward.1 = (bf16[512,3072]{1,0:T(8,128)(2,1)}, f32[5,8,3072]{2,1,0:T(8,128)}, bf16[512,256]{1,0:T(8,128)(2,1)}, f32[5,8,256]{2,1,0:T(8,128)}, bf16[512,128]{1,0:T(8,128)(2,1)}, /*index=5*/f32[3,8,128]{2,1,0:T(8,128)}) custom-call(bf16[512,3072]{1,0:T(8,128)(2,1)} %get-tuple-element.33.dy_ref, bf16[512,3072]{1,0:T(8,128)(2,1)} %get-tuple-element.34.x_ref, ...), custom_call_target="tpu_custom_call" | custom-call | flops 40000000000 | bytes 20000000 | tf_op jit(solution)/shard_map/scan_backward/pallas_call | solution.py:486
  344.4 3.3 convolution_convert_fusion
  348.4 8.4 %collective-permute-done.10 = bf16[768,3456]{1,0:T(8,128)(2,1)S(1)} collective-permute-done((bf16[768,3456]{1,0:T(8,128)(2,1)S(1)}, bf16[768,3456]{1,0:T(8,128)(2,1)S(1)}, u32[]{:S(2)}, u32[]{:S(2)}) %collective-permute-start.10) | collective-permute-done | bytes 5308448 | tf_op jit(solution)/shard_map/ppermute | solution.py:622
  356.8 4.9 add_convert_fusion
  364.3 6.1 fusion.23
  370.4 5.7 fusion.24
  376.2 5.2 convolution_add_fusion
  382.6 4.5 multiply_reduce_fusion.1
  387.2 11.2 %reduce-scatter.8.cloned.1.call-done = bf16[768,768]{1,0:T(8,128)(2,1)} async-done(((bf16[3072,768]{1,0:T(8,128)(2,1)}), bf16[768,768]{1,0:T(8,128)(2,1)}) %reduce-scatter.8.cloned.1.call-update) | async-done | bytes 1179664 | tf_op jit(solution)/shard_map/reduce_scatter | solution.py:718
  398.3 65.3 %reduce-scatter.6.cloned.1.call-done = bf16[192,3456]{1,0:T(8,128)(2,1)} async-done(((bf16[768,3456]{1,0:T(8,128)(2,1)}), bf16[192,3456]{1,0:T(8,128)(2,1)}) %reduce-scatter.6.cloned.1.call-update) | async-done | bytes 1327120 | tf_op jit(solution)/shard_map/reduce_scatter | solution.py:718
  465.4 6.1 add_convert_fusion.7
  471.5 6.9 %broadcast_select_fusion.9 = (bf16[512,768]{1,0:T(8,128)(2,1)}, bf16[512,768]{1,0:T(8,128)(2,1)}) fusion(bf16[512,768]{1,0:T(8,128)(2,1)S(1)} %add_convert_fusion.7, pred[]{:T(512)S(6)} %eq.93, f32[512,768]{1,0:T(8,128)S(1)} %copy-done.3, bf16[512,3072]{1,0:T(8,128)(2,1)S(1)} %copy-done.39, bf16[3072,768]{0,1:T(8,128)(2,1)} %collective-permute-done.2), kind=kOutput, calls=%fused_computation.48 | convolution fusion | flops 2417491968 | bytes 11796481 | tf_op jit(solution)/shard_map/dot_general | solution.py:20
  480.0 3.3 collective-permute-done.4
  484.9 2.5 broadcast_select_fusion.7
  487.4 3.1 copy.135
  492.7 112.0 %all-reduce.11.cloned.1.call-done = (bf16[192,3456]{1,0:T(8,128)(2,1)}, bf16[192,3072]{1,0:T(8,128)(2,1)}, bf16[768,768]{1,0:T(8,128)(2,1)}) async-done(((bf16[192,3456]{1,0:T(8,128)(2,1)}, bf16[192,3072]{1,0:T(8,128)(2,1)}, bf16[768,768]{1,0:T(8,128)(2,1)}), (bf16[192,3456]{1,0:T(8,128)(2,1)}, bf16[192,3072]{1,0:T(8,128)(2,1)}, bf16[768,768]{1,0:T(8,128)(2,1)})) %all-reduce.11.cloned.1.call-update) | async-done | bytes 3686416 | tf_op jit(solution)/shard_map/psum | solution.py:719
  604.8 2.4 pad_maximum_fusion
  607.2 2.3 copy.126
  617.3 2.6 copy.142
  622.1 3.6 copy.143
  626.7 7.8 %rev.3 = f32[4,3328]{1,0:T(4,128)} reverse(f32[4,3328]{1,0:T(4,128)S(1)} %slice.103), dimensions={0} | reverse | bytes 106496 | tf_op jit(solution)/shard_map/rev | solution.py:774
  640.4 2.5 copy.141
  642.9 6.0 copy.145
  652.7 19.8 %maximum_convert_fusion = f32[384,6448]{1,0:T(8,128)} fusion(bf16[192,3376]{1,0:T(8,128)(2,1)S(1)} %get-tuple-element.120, bf16[192,3072]{1,0:T(8,128)(2,1)S(1)} %get-tuple-element.124, bf16[192,3376]{1,0:T(8,128)(2,1)S(1)} %get-tuple-element.119, bf16[192,3072]{1,0:T(8,128)(2,1)S(1)} %get-tuple-element.123), kind=kLoop, calls=%fused_computation.11 | loop fusion | flops 19808256 | bytes 14856192 | tf_op jit(solution)/shard_map/convert_element_type | solution.py:767
  672.5 10.7 %copy.144 = f32[384,6448]{0,1:T(8,128)} copy(f32[384,6448]{1,0:T(8,128)} %maximum_convert_fusion) | data formatting | bytes 19808256
  (222 shorter events, 60.6 us)
Async XLA Ops:
  7.2 62.3 %all-gather.6.cloned.1.call-start = ((), (), s32[]{:S(2)}) async-start(), calls=%async_computation.4 | async-start | bytes 5898240 | tf_op jit(solution)/shard_map/all_gather | solution.py:682
  11.2 117.1 %all-gather.8.cloned.1.call-start = ((), (), s32[]{:S(2)}) async-start(), calls=%async_computation.5 | async-start | bytes 5898240 | tf_op jit(solution)/shard_map/all_gather | solution.py:685
  15.2 177.4 %all-gather.4.cloned.1.call-start = ((), (), s32[]{:S(2)}) async-start(), calls=%async_computation.3 | async-start | bytes 6635520 | tf_op jit(solution)/shard_map/all_gather | solution.py:680
  20.4 366.8 %reduce-scatter.4.cloned.1.call-start = ((), (), s32[]{:S(2)}) async-start(), calls=%async_computation.6 | async-start | bytes 5898240 | tf_op jit(solution)/shard_map/reduce_scatter | solution.py:718
  26.3 6.5 copy-start.33
  26.3 7.3 %copy-start.29 = (s32[512]{0:T(512)S(1)}, s32[512]{0:T(512)}, u32[]{:S(2)}) copy-start(s32[512]{0:T(512)} %param.13) | copy-start | bytes 6148
  28.3 100.1 %copy-start = (f32[512,768]{1,0:T(8,128)}, f32[512,768]{1,0:T(8,128)S(1)}, u32[]{:S(2)}) copy-start(f32[512,768]{1,0:T(8,128)S(1)} %copy.123) | copy-start | bytes 4718596
  32.1 96.2 %copy-start.23 = (f32[768]{0:T(1024)}, f32[768]{0:T(1024)S(1)}, u32[]{:S(2)}) copy-start(f32[768]{0:T(1024)S(1)} %mul.160) | copy-start | bytes 9220
  32.2 96.1 %copy-start.25 = (f32[768]{0:T(1024)}, f32[768]{0:T(1024)S(1)}, u32[]{:S(2)}) copy-start(f32[768]{0:T(1024)S(1)} %mul.155) | copy-start | bytes 9220
  33.6 35.9 %copy-start.34 = (f32[48]{0:T(128)S(1)}, f32[48]{0:T(128)}, u32[]{:S(2)}) copy-start(f32[48]{0:T(128)} %param.19) | copy-start | bytes 580
  33.6 35.9 %copy-start.35 = (f32[48]{0:T(128)S(1)}, f32[48]{0:T(128)}, u32[]{:S(2)}) copy-start(f32[48]{0:T(128)} %param.18) | copy-start | bytes 580
  35.2 93.1 %copy-start.2 = (f32[512,768]{1,0:T(8,128)S(1)}, f32[512,768]{1,0:T(8,128)}, u32[]{:S(2)}) copy-start(f32[512,768]{1,0:T(8,128)} %copy.120) | copy-start | bytes 4718596
  38.7 91.1 %copy-start.27 = (f32[512]{0:T(512)}, f32[512]{0:T(512)S(1)}, u32[]{:S(2)}) copy-start(f32[512]{0:T(512)S(1)} %add_rsqrt_fusion) | copy-start | bytes 6148
  69.5 136.0 %collective-permute-start.1 = (bf16[768,3072]{1,0:T(8,128)(2,1)}, bf16[768,3072]{1,0:T(8,128)(2,1)}, u32[]{:S(2)}, u32[]{:S(2)}) collective-permute-start(bf16[768,3072]{1,0:T(8,128)(2,1)} %all-gather.6.cloned.1.call-done), channel_id=1, source_target_pairs={{0,4},{4,0},{1,5},{5,1},{2,6},{6,2},{3,7},{7,3},{8,12},{12,8},{9,1... | collective-permute-start | bytes 14155784 | tf_op jit(solution)/shard_map/ppermute | solution.py:622
  128.3 83.8 %collective-permute-start.2 = (bf16[3072,768]{0,1:T(8,128)(2,1)}, bf16[3072,768]{0,1:T(8,128)(2,1)}, u32[]{:S(2)}, u32[]{:S(2)}) collective-permute-start(bf16[3072,768]{0,1:T(8,128)(2,1)} %all-gather.8.cloned.1.call-done), channel_id=1, source_target_pairs={{0,4},{4,0},{1,5},{5,1},{2,6},{6,2},{3,7},{7,3},{8,12},{12,8},{9,1... | collective-permute-start | bytes 14155784 | tf_op jit(solution)/shard_map/ppermute | solution.py:622
  129.8 65.2 %copy-start.6 = (bf16[512,768]{1,0:T(8,128)(2,1)S(1)}, bf16[512,768]{1,0:T(8,128)(2,1)}, u32[]{:S(2)}) copy-start(bf16[512,768]{1,0:T(8,128)(2,1)} %get-tuple-element.141) | copy-start | bytes 2359300
  192.6 26.1 %collective-permute-start = (bf16[768,3456]{1,0:T(8,128)(2,1)}, bf16[768,3456]{1,0:T(8,128)(2,1)}, u32[]{:S(2)}, u32[]{:S(2)}) collective-permute-start(bf16[768,3456]{1,0:T(8,128)(2,1)} %all-gather.4.cloned.1.call-done), channel_id=1, source_target_pairs={{0,4},{4,0},{1,5},{5,1},{2,6},{6,2},{3,7},{7,3},{8,12},{12,8},{9,1... | collective-permute-start | bytes 15925256 | tf_op jit(solution)/shard_map/ppermute | solution.py:622
  195.0 7.4 %slice-start = ((s8[5308416]{0:T(1024)(128)(4,1)}), s8[4194304]{0:T(1024)(128)(4,1)S(1)}, s32[]{:S(2)}) async-start(s8[5308416]{0:T(1024)(128)(4,1)} %bitcast.116), calls=%async_computation.10 | async-start | bytes 8388608
  205.5 6.6 copy-start.4
  264.0 13.0 %copy-start.36 = (bf16[512,3072]{1,0:T(8,128)(2,1)S(1)}, bf16[512,3072]{1,0:T(8,128)(2,1)}, u32[]{:S(2)}) copy-start(bf16[512,3072]{1,0:T(8,128)(2,1)} %get-tuple-element.32) | copy-start | bytes 9437188
  268.9 8.1 %collective-permute-start.8 = (bf16[768,3072]{1,0:T(8,128)(2,1)S(1)}, bf16[768,3072]{1,0:T(8,128)(2,1)S(1)}, u32[]{:S(2)}, u32[]{:S(2)}) collective-permute-start(bf16[768,3072]{1,0:T(8,128)(2,1)S(1)} %convolution_convert_fusion.2), channel_id=1, source_target_pairs={{0,4},{4,0},{1,5},{5,1},{2,6},{6,2},{3,7},{7,3},{8,12},{12,8},{9,1... | collective-permute-start | bytes 14155784 | tf_op jit(solution)/shard_map/ppermute | solution.py:622
  281.3 117.0 %reduce-scatter.8.cloned.1.call-start = ((), (), s32[]{:S(2)}) async-start(), calls=%async_computation.8 | async-start | bytes 5898240 | tf_op jit(solution)/shard_map/reduce_scatter | solution.py:718
  286.0 8.0 %copy-start.38 = (bf16[512,3072]{1,0:T(8,128)(2,1)S(1)}, bf16[512,3072]{1,0:T(8,128)(2,1)}, u32[]{:S(2)}) copy-start(bf16[512,3072]{1,0:T(8,128)(2,1)} %get-tuple-element.31) | copy-start | bytes 9437188
  286.0 8.0 %collective-permute-start.12 = (bf16[3072,768]{1,0:T(8,128)(2,1)S(1)}, bf16[3072,768]{1,0:T(8,128)(2,1)S(1)}, u32[]{:S(2)}, u32[]{:S(2)}) collective-permute-start(bf16[3072,768]{1,0:T(8,128)(2,1)S(1)} %convolution_convert_fusion.1), channel_id=1, source_target_pairs={{0,4},{4,0},{1,5},{5,1},{2,6},{6,2},{3,7},{7,3},{8,12},{12,8},{9,1... | collective-permute-start | bytes 14155784 | tf_op jit(solution)/shard_map/ppermute | solution.py:622
  298.3 165.4 %reduce-scatter.6.cloned.1.call-start = ((), (), s32[]{:S(2)}) async-start(), calls=%async_computation.7 | async-start | bytes 6635520 | tf_op jit(solution)/shard_map/reduce_scatter | solution.py:718
  344.4 12.4 %copy-start.11 = (bf16[512,3456]{1,0:T(8,128)(2,1)}, bf16[512,3456]{1,0:T(8,128)(2,1)S(1)}, u32[]{:S(2)}) copy-start(bf16[512,3456]{1,0:T(8,128)(2,1)S(1)} %constant_dynamic-update-slice_fusion) | copy-start | bytes 10616836
  347.7 9.0 %collective-permute-start.10 = (bf16[768,3456]{1,0:T(8,128)(2,1)S(1)}, bf16[768,3456]{1,0:T(8,128)(2,1)S(1)}, u32[]{:S(2)}, u32[]{:S(2)}) collective-permute-start(bf16[768,3456]{1,0:T(8,128)(2,1)S(1)} %convolution_convert_fusion), channel_id=1, source_target_pairs={{0,4},{4,0},{1,5},{5,1},{2,6},{6,2},{3,7},{7,3},{8,12},{12,8},{9,1... | collective-permute-start | bytes 15925256 | tf_op jit(solution)/shard_map/ppermute | solution.py:622
  361.7 243.1 %all-reduce.11.cloned.1.call-start = ((), (), s32[]{:S(2)}) async-start(), calls=%async_computation.9 | async-start | bytes 7372800 | tf_op jit(solution)/shard_map/psum | solution.py:719
  364.3 18.3 %slice-start.2 = ((s8[5308416]{0:T(1024)(128)(4,1)}), s8[4194304]{0:T(1024)(128)(4,1)S(1)}, s32[]{:S(2)}) async-start(s8[5308416]{0:T(1024)(128)(4,1)} %bitcast.118), calls=%async_computation.12 | async-start | bytes 8388608
  370.4 12.1 %slice-start.3 = ((s8[5308416]{0:T(1024)(128)(4,1)}), s8[1114112]{0:T(1024)(128)(4,1)S(1)}, s32[]{:S(2)}) async-start(s8[5308416]{0:T(1024)(128)(4,1)} %bitcast.118), calls=%async_computation.13 | async-start | bytes 2228224
  376.1 6.4 copy-start.1
  376.1 6.4 copy-start.3
  387.1 76.8 %copy-start.21 = (f32[8,3072]{1,0:T(8,128)S(1)}, f32[8,3072]{1,0:T(8,128)}, u32[]{:S(2)}) copy-start(f32[8,3072]{1,0:T(8,128)} %get-tuple-element.48) | copy-start | bytes 294916
  387.1 76.9 %copy-start.31 = (f32[3,8,128]{2,1,0:T(8,128)S(1)}, f32[3,8,128]{2,1,0:T(8,128)}, u32[]{:S(2)}) copy-start(f32[3,8,128]{2,1,0:T(8,128)} %get-tuple-element.47) | copy-start | bytes 36868
  387.1 76.9 %copy-start.22 = (f32[5,8,256]{2,1,0:T(8,128)S(1)}, f32[5,8,256]{2,1,0:T(8,128)}, u32[]{:S(2)}) copy-start(f32[5,8,256]{2,1,0:T(8,128)} %get-tuple-element.46) | copy-start | bytes 122884
  465.3 13.1 %collective-permute-start.3 = (f32[176,128]{1,0:T(8,128)S(1)}, f32[176,128]{1,0:T(8,128)S(1)}, u32[]{:S(2)}, u32[]{:S(2)}) collective-permute-start(f32[176,128]{1,0:T(8,128)S(1)} %fusion.7), channel_id=1, source_target_pairs={{0,4},{4,0},{1,5},{5,1},{2,6},{6,2},{3,7},{7,3},{8,12},{12,8},{9,1... | collective-permute-start | bytes 270344 | tf_op jit(solution)/shard_map/ppermute | solution.py:629
  471.5 13.4 %copy-start.9 = (bf16[512,768]{1,0:T(8,128)(2,1)S(1)}, bf16[512,768]{1,0:T(8,128)(2,1)}, u32[]{:S(2)}) copy-start(bf16[512,768]{1,0:T(8,128)(2,1)} %copy.128) | copy-start | bytes 2359300
  471.5 13.4 %copy-start.10 = (bf16[512,768]{1,0:T(8,128)(2,1)S(1)}, bf16[512,768]{1,0:T(8,128)(2,1)}, u32[]{:S(2)}) copy-start(bf16[512,768]{1,0:T(8,128)(2,1)} %copy.132) | copy-start | bytes 2359300
  471.5 13.4 %copy-start.15 = (f32[512,768]{1,0:T(8,128)S(1)}, f32[512,768]{1,0:T(8,128)}, u32[]{:S(2)}) copy-start(f32[512,768]{1,0:T(8,128)} %copy-done.14) | copy-start | bytes 4718596
  471.5 13.4 %copy-start.16 = (f32[512,768]{1,0:T(8,128)S(1)}, f32[512,768]{1,0:T(8,128)}, u32[]{:S(2)}) copy-start(f32[512,768]{1,0:T(8,128)} %get-tuple-element.148) | copy-start | bytes 4718596
  478.5 4.8 collective-permute-start.4
  483.3 8.8 %collective-permute-start.5 = (f32[176,128]{1,0:T(8,128)S(1)}, f32[176,128]{1,0:T(8,128)S(1)}, u32[]{:S(2)}, u32[]{:S(2)}) collective-permute-start(f32[176,128]{1,0:T(8,128)S(1)} %fusion.62), channel_id=1, source_target_pairs={{0,2},{1,3},{2,0},{3,1},{4,6},{5,7},{6,4},{7,5},{8,10},{9,11},{10,... | collective-permute-start | bytes 270344 | tf_op jit(solution)/shard_map/ppermute | solution.py:629
  492.1 119.6 %collective-permute-start.6 = (f32[176,128]{1,0:T(8,128)S(1)}, f32[176,128]{1,0:T(8,128)S(1)}, u32[]{:S(2)}, u32[]{:S(2)}) collective-permute-start(f32[176,128]{1,0:T(8,128)S(1)} %add.158), channel_id=1, source_target_pairs={{0,8},{8,0},{16,24},{24,16},{1,9},{9,1},{17,25},{25,17},{2,10},{10... | collective-permute-start | bytes 270344 | tf_op jit(solution)/shard_map/ppermute | solution.py:629
  604.8 32.6 %collective-permute-start.13 = (bf16[768,768]{1,0:T(8,128)(2,1)}, bf16[768,768]{1,0:T(8,128)(2,1)}, u32[]{:S(2)}, u32[]{:S(2)}) collective-permute-start(bf16[768,768]{1,0:T(8,128)(2,1)} %get-tuple-element.116), channel_id=1, source_target_pairs={{0,4},{4,0},{1,5},{5,1},{2,6},{6,2},{3,7},{7,3},{8,12},{12,8},{9,1... | collective-permute-start | bytes 3538952 | tf_op jit(solution)/shard_map/ppermute | solution.py:622
  612.4 13.3 %collective-permute-start.7 = (f32[176,128]{1,0:T(8,128)}, f32[176,128]{1,0:T(8,128)}, u32[]{:S(2)}, u32[]{:S(2)}) collective-permute-start(f32[176,128]{1,0:T(8,128)} %add.159), channel_id=1, source_target_pairs={{0,16},{8,24},{16,0},{24,8},{1,17},{9,25},{17,1},{25,9},{2,18},{10... | collective-permute-start | bytes 270344 | tf_op jit(solution)/shard_map/ppermute | solution.py:629
  622.1 15.2 %copy-start.17 = (bf16[768,768]{1,0:T(8,128)(2,1)S(1)}, bf16[768,768]{1,0:T(8,128)(2,1)}, u32[]{:S(2)}) copy-start(bf16[768,768]{1,0:T(8,128)(2,1)} %get-tuple-element.116) | copy-start | bytes 3538948
  635.1 13.8 %collective-permute-start.9 = (bf16[192,3072]{1,0:T(8,128)(2,1)}, bf16[192,3072]{1,0:T(8,128)(2,1)}, u32[]{:S(2)}, u32[]{:S(2)}) collective-permute-start(bf16[192,3072]{1,0:T(8,128)(2,1)} %get-tuple-element.115), channel_id=1, source_target_pairs={{0,4},{4,0},{1,5},{5,1},{2,6},{6,2},{3,7},{7,3},{8,12},{12,8},{9,1... | collective-permute-start | bytes 3538952 | tf_op jit(solution)/shard_map/ppermute | solution.py:622
  637.0 13.7 %collective-permute-start.11 = (bf16[192,3456]{1,0:T(8,128)(2,1)}, bf16[192,3456]{1,0:T(8,128)(2,1)}, u32[]{:S(2)}, u32[]{:S(2)}) collective-permute-start(bf16[192,3456]{1,0:T(8,128)(2,1)} %get-tuple-element.114), channel_id=1, source_target_pairs={{0,4},{4,0},{1,5},{5,1},{2,6},{6,2},{3,7},{7,3},{8,12},{12,8},{9,1... | collective-permute-start | bytes 3981320 | tf_op jit(solution)/shard_map/ppermute | solution.py:622
  (17 other events, 74.7 us)
Sparse Core Ops, SparseCore 0:
  11.3 58.1 all-gather.5
  71.3 56.9 all-gather.7
  130.7 61.8 all-gather.3
  281.5 56.9 reduce-scatter.3
  341.3 56.9 reduce-scatter.7
  401.8 61.8 reduce-scatter.5
  466.3 138.4 all-reduce.10

commit v2 on v1

--- a/solution.py
+++ b/solution.py
@@ -6,6 +6,7 @@
 from jax.experimental import pallas as pl
 from jax.experimental.pallas import tpu as pltpu
 from jax.sharding import Mesh, PartitionSpec as P
+
 
 EPS = 1e-05
 HIGHEST = lax.Precision.HIGHEST
@@ -226,7 +227,7 @@
     )
 
 
-def norm_kernel(y_ref, z_ref, dm_ref, gain, live_ref, mixer_out, d_y, d_z, gg_out, gated_s, slope_s):
+def norm_kernel(taps, y_ref, z_ref, dm_ref, gain, live_ref, mixer_out, d_y, d_z, gg_out, gated_s, gg_s):
     rows = y_ref.shape[0]
     inner = y_ref.shape[1]
     tiles = inner // 128
@@ -248,7 +249,7 @@
 
     @pl.when(pl.program_id(0) == 0)
     def _():
-        gg_out[...] = jnp.zeros_like(gg_out)
+        gg_s[...] = jnp.zeros_like(gg_s)
 
     for t in range(tiles):
         lanes = slice(t * 128, t * 128 + 128)
@@ -260,18 +261,23 @@
         scale = gain[:, lanes]
         mixer_out[:, lanes] = (gated * keep * scale).astype(BF16)
         m = dm_ref[:, lanes].astype(F32) * keep
-        gg_out[:, lanes] += jnp.sum((m * gated).reshape(rows // 8, 8, 128), axis=0)
+        gg_s[:, lanes] += jnp.sum((m * gated).reshape(rows // 8, 8, 128), axis=0)
         d_gated = m * scale - gated * back
         d_y[:, lanes] = (d_gated * gate).astype(BF16)
         d_z[:, lanes] = (d_gated * y_ref[:, lanes].astype(F32) * slope).astype(BF16)
 
-
-def run_norm(y, z, d_mixer, gain, live):
+    @pl.when(pl.program_id(0) == pl.num_programs(0) - 1)
+    def _():
+        line = lax.broadcasted_iota(jnp.int32, gg_out.shape, 0)
+        gg_out[...] = jnp.where(line == taps + 1, jnp.sum(gg_s[...], axis=0, keepdims=True), 0.0)
+
+
+def run_norm(y, z, d_mixer, gain, live, taps):
     rows, inner = y.shape
     block = 128
     spec = pl.BlockSpec((block, inner), lambda i: (i, 0))
     return pl.pallas_call(
-        norm_kernel,
+        partial(norm_kernel, taps),
         grid=(rows // block,),
         in_specs=[
             spec, spec, spec,
@@ -285,7 +291,7 @@
             jax.ShapeDtypeStruct((rows, inner), BF16),
             jax.ShapeDtypeStruct((8, inner), F32),
         ),
-        scratch_shapes=[pltpu.VMEM((block, inner), F32), pltpu.VMEM((block, 128), F32)],
+        scratch_shapes=[pltpu.VMEM((block, inner), F32), pltpu.VMEM((8, inner), F32)],
         cost_estimate=pl.CostEstimate(
             flops=10_000_000_000, bytes_accessed=20_000_000, transcendentals=0
         ),
@@ -299,30 +305,50 @@
     d0 = window[0:LC, :]
     fold = lambda v: jnp.sum(v.reshape(LC // 8, 8, 128), axis=0)
     result = weight[taps - 1 : taps, :] * d0
-    sums = [fold(d0), fold(d0 * x)]
+    sums = [fold(d0 * x)]
     for offset in range(1, taps):
         moved = window[offset : offset + LC, :] * masks[offset - 1, pl.ds(row, LC), :]
         result = result + weight[taps - 1 - offset : taps - offset, :] * moved
-        sums.append(fold(moved * x))
-    return result, sums
+        sums.insert(0, fold(moved * x))
+    return result, sums + [fold(d0)]
+
+
+KEPT = 7
+
+
+def fold_rows(sums, width):
+    line = lax.broadcasted_iota(jnp.int32, (8, width), 0)
+    result = jnp.zeros((8, width), F32)
+    for k in range(sums.shape[0]):
+        result = jnp.where(line == k, jnp.sum(sums[k], axis=0, keepdims=True), result)
+    return result
 
 
 def backward_kernel(
-    head_count,
+    head_count, first_group, opens, closes,
     dy_ref, x_ref, slope_ref, x_in, bc_in, s0_ref, bc_ref, bcs_ref, stack, heads, at_ref, dt_in,
     wx, wbc, dt_bias, a_log, skip, um_ref, allowed_t, ex, exa, hs,
-    dx_out, sums_out, dbc_out, sums_bc_out, ddt_out, small_out,
-    padded, grad, cbt, dcbt, ct, d_writer, d_reader, prow, qcol, hsum, sgrow,
-    d1, ea, ew, ax, inter, gb, dye, xdt, xw, sacc,
+    *rest,
 ):
+    kept_in, rest = ((), rest) if opens else (rest[:KEPT], rest[KEPT:])
+    dx_out, sums_out, rest = rest[0], rest[1], rest[2:]
+    if closes:
+        (dbc_out, sums_bc_out, ddt_out, small_out), rest = rest[:4], rest[4:]
+        kept, rest = rest[:KEPT], rest[KEPT:]
+    else:
+        kept, rest = rest[:KEPT], rest[KEPT:]
+    dcbt, d_writer, d_reader, prow, qcol, hsum, sgrow = kept
+    (
+        padded, sums_s, grad, cbt, ct, d1, ea, ew, ax, inter, gb, dye, xdt, xw, sacc,
+    ) = rest
     rows = x_ref.shape[0]
     chunks = rows // LC
     width = x_ref.shape[1]
     taps = wx.shape[0]
-    group = pl.program_id(0)
+    group = pl.program_id(0) + first_group
     tiles = width // 128
 
-    @pl.when(group == 0)
+    @pl.when(pl.program_id(0) == 0)
     def _():
         padded[rows:, :] = jnp.zeros((8, width), F32)
         for c in range(chunks):
@@ -331,8 +357,8 @@
             reader = bc_ref[here, 128:256]
             cbt[here, :] = dot(writer, reader, NT) * allowed_t[here, :]
             ct[:, here] = reader.astype(F32).T.astype(BF16)
-        for ref in (dcbt, d_writer, d_reader, prow, qcol, hsum, sgrow):
-            ref[...] = jnp.zeros_like(ref)
+        for index, ref in enumerate(kept):
+            ref[...] = jnp.zeros_like(ref) if opens else kept_in[index][...]
 
     grad[...] = jnp.zeros_like(grad)
     low = lax.broadcasted_iota(jnp.int32, (LC, 128), 1) < HD
@@ -408,7 +434,7 @@
 
     lax.fori_loop(0, chunks, chunk, 0)
 
-    sums_out[...] = jnp.zeros_like(sums_out)
+    sums_s[...] = jnp.zeros_like(sums_s)
 
     def conv_chunk(c, carry):
         row = pl.multiple_of(c * LC, LC)
@@ -417,12 +443,15 @@
             result, sums = conv_backward(padded, row, lanes, x_in, wx[:, lanes], taps, um_ref)
             dx_out[pl.ds(row, LC), lanes] = result.astype(BF16)
             for k in range(taps + 1):
-                sums_out[k, :, lanes] += sums[k]
+                sums_s[k, :, lanes] += sums[k]
         return carry
 
     lax.fori_loop(0, chunks, conv_chunk, 0)
-
-    @pl.when(group == pl.num_programs(0) - 1)
+    sums_out[...] = fold_rows(sums_s[...], width)
+    if not closes:
+        return
+
+    @pl.when(pl.program_id(0) == pl.num_programs(0) - 1)
     def _():
         total_a = jnp.zeros((8, 128), F32)
         total_dt = jnp.zeros((8, 128), F32)
@@ -433,7 +462,7 @@
         ).astype(F32)
         at_end = lax.broadcasted_iota(jnp.int32, (LC, 128), 0) == LC - 1
         fold = lambda v: jnp.sum(v.reshape(LC // 8, 8, 128), axis=0)
-        sums_bc_out[...] = jnp.zeros_like(sums_bc_out)
+        sums_s[...] = jnp.zeros_like(sums_s)
         for c in range(chunks):
             here = slice(c * LC, c * LC + LC)
             writer = bc_ref[here, 0:128]
@@ -459,9 +488,11 @@
             total_dt = total_dt + fold(d_raw)
             total_a = total_a + fold(d_decay * decay)
             total_skip = total_skip + fold(hsum[3, here, :])
-        small_out[0] = total_dt
-        small_out[1] = total_a
-        small_out[2] = total_skip
+        line = lax.broadcasted_iota(jnp.int32, (8, 128), 0)
+        result = jnp.zeros((8, 128), F32)
+        for k, total in enumerate((total_dt, total_a, total_skip)):
+            result = jnp.where(line == k, jnp.sum(total, axis=0, keepdims=True), result)
+        small_out[...] = result
         for c in range(chunks):
             row = c * LC
             for p in range(2):
@@ -469,30 +500,69 @@
                 result, sums = conv_backward(padded, row, lanes, bc_in, wbc[:, lanes], taps, um_ref)
                 dbc_out[row : row + LC, lanes] = result.astype(BF16)
                 for k in range(taps + 1):
-                    sums_bc_out[k, :, lanes] += sums[k]
-
-
-def run_backward(dy, saved, proj, head_count, state_dim, conv_w, dt_bias, a_log, skip, masks):
+                    sums_s[k, :, lanes] += sums[k]
+        sums_bc_out[...] = fold_rows(sums_s[:, :, 0:256], 256)
+
+
+def run_backward(
+    dy, saved, proj, head_count, state_dim, conv_w, dt_bias, a_log, skip, masks, span, kept=None
+):
     x, slope, _, s0, bc_val, bc_slope, stack, heads, at = saved
     rows, inner = dy.shape
     chunks = rows // LC
     width = HEADS_STEP * HD
-    groups = inner // width
+    first, last = span
+    opens, closes = first == 0, last == inner // width
     taps = conv_w.shape[0]
     bc = 2 * state_dim
     const = lambda *index: (lambda g: index)
     full = lambda shape: pl.BlockSpec(shape, lambda g: (0,) * len(shape))
-    col = lambda lead: pl.BlockSpec((lead, width), lambda g: (0, g))
+    col = lambda lead: pl.BlockSpec((lead, width), lambda g: (0, g + first))
+    own = lambda lead: pl.BlockSpec((lead, width), lambda g: (0, g))
+    kept_shapes = [
+        (rows, 128), (rows, 128), (rows, 128), (chunks, 128, LC), (rows, 128), (4, rows, 128),
+        (chunks * 8, 128),
+    ]
+    out_specs = [own(rows), own(8)]
+    out_shape = [
+        jax.ShapeDtypeStruct((rows, (last - first) * width), BF16),
+        jax.ShapeDtypeStruct((8, (last - first) * width), F32),
+    ]
+    scratch = [
+        pltpu.VMEM((rows + 8, width), F32),
+        pltpu.VMEM((taps + 1, 8, width), F32),
+        pltpu.VMEM((state_dim, width), F32),
+        pltpu.VMEM((rows, 128), F32),
+        pltpu.VMEM((state_dim, rows), BF16),
+        pltpu.VMEM((LC, width), F32),
+        pltpu.VMEM((LC, width), F32),
+        pltpu.VMEM((LC, width), F32),
+        pltpu.VMEM((LC, HEADS_STEP * 128), F32),
+        pltpu.VMEM((LC, width), F32),
+        pltpu.VMEM((LC, width), F32),
+        pltpu.VMEM((LC, width), BF16),
+        pltpu.VMEM((LC, width), BF16),
+        pltpu.VMEM((LC, width), BF16),
+        pltpu.VMEM((4, LC, width), BF16),
+    ]
+    if closes:
+        shapes = [((rows, bc), BF16), ((8, bc), F32), ((rows, 128), BF16), ((8, 128), F32)]
+        scratch = [pltpu.VMEM(shape, F32) for shape in kept_shapes] + scratch
+    else:
+        shapes = [(shape, F32) for shape in kept_shapes]
+    out_specs += [full(shape) for shape, _ in shapes]
+    out_shape += [jax.ShapeDtypeStruct(shape, kind) for shape, kind in shapes]
+    share = (last - first) * width / inner
     return pl.pallas_call(
-        partial(backward_kernel, head_count),
-        grid=(groups,),
+        partial(backward_kernel, head_count, first, opens, closes),
+        grid=(last - first,),
         in_specs=[
             col(rows),
             col(rows),
             col(rows),
             col(rows),
             pl.BlockSpec((rows, bc), const(0, inner // bc)),
-            pl.BlockSpec((chunks, state_dim, width), lambda g: (0, 0, g)),
+            pl.BlockSpec((chunks, state_dim, width), lambda g: (0, 0, g + first)),
             full((rows, bc)),
             full((rows, bc)),
             full((4, rows, 256)),
@@ -507,57 +577,86 @@
             full((taps - 1, rows, 128)),
             full((rows, 128)),
             col(256),
-            pl.BlockSpec((256, HEADS_STEP * 128), lambda g: (0, g)),
-            pl.BlockSpec((width, 128), lambda g: (g, 0)),
-        ],
-        out_specs=[
-            col(rows),
-            pl.BlockSpec((taps + 1, 8, width), lambda g: (0, 0, g)),
-            full((rows, bc)),
-            full((taps + 1, 8, bc)),
-            full((rows, 128)),
-            full((3, 8, 128)),
-        ],
-        out_shape=(
-            jax.ShapeDtypeStruct((rows, inner), BF16),
-            jax.ShapeDtypeStruct((taps + 1, 8, inner), F32),
-            jax.ShapeDtypeStruct((rows, bc), BF16),
-            jax.ShapeDtypeStruct((taps + 1, 8, bc), F32),
-            jax.ShapeDtypeStruct((rows, 128), BF16),
-            jax.ShapeDtypeStruct((3, 8, 128), F32),
-        ),
-        scratch_shapes=[
-            pltpu.VMEM((rows + 8, width), F32),
-            pltpu.VMEM((state_dim, width), F32),
-            pltpu.VMEM((rows, 128), F32),
-            pltpu.VMEM((rows, 128), F32),
-            pltpu.VMEM((state_dim, rows), BF16),
-            pltpu.VMEM((rows, 128), F32),
-            pltpu.VMEM((rows, 128), F32),
-            pltpu.VMEM((chunks, 128, LC), F32),
-            pltpu.VMEM((rows, 128), F32),
-            pltpu.VMEM((4, rows, 128), F32),
-            pltpu.VMEM((chunks * 8, 128), F32),
-            pltpu.VMEM((LC, width), F32),
-            pltpu.VMEM((LC, width), F32),
-            pltpu.VMEM((LC, width), F32),
-            pltpu.VMEM((LC, HEADS_STEP * 128), F32),
-            pltpu.VMEM((LC, width), F32),
-            pltpu.VMEM((LC, width), F32),
-            pltpu.VMEM((LC, width), BF16),
-            pltpu.VMEM((LC, width), BF16),
-            pltpu.VMEM((LC, width), BF16),
-            pltpu.VMEM((4, LC, width), BF16),
-        ],
+            pl.BlockSpec((256, HEADS_STEP * 128), lambda g: (0, g + first)),
+            pl.BlockSpec((width, 128), lambda g: (g + first, 0)),
+        ]
+        + ([] if opens else [full(shape) for shape in kept_shapes]),
+        out_specs=out_specs,
+        out_shape=out_shape,
+        scratch_shapes=scratch,
         cost_estimate=pl.CostEstimate(
-            flops=40_000_000_000, bytes_accessed=20_000_000, transcendentals=0
+            flops=int(40e9 * share), bytes_accessed=int(20e6 * share), transcendentals=0
         ),
         name="scan_backward",
     )(
         dy, x, slope, proj, proj, s0, bc_val, bc_slope, stack, heads, at, proj,
         conv_w, conv_w, dt_bias, a_log, skip, masks["um"], masks["allowed_t"],
-        masks["ex"], masks["exa"], masks["hs"],
-    )
+        masks["ex"], masks["exa"], masks["hs"], *(() if opens else kept),
+    )
+
+
+def join_kernel(axis, core_ref, *refs):
+    out = refs[-1]
+    own = (pl.program_id(0) // axis == core_ref[0]).astype(F32)
+    at = 0
+    for mine, other in zip(refs[0:-1:2], refs[1:-1:2]):
+        width = min(mine.shape[1], out.shape[1] - at)
+        value = jnp.where(own > 0.5, mine[:, 0:width].astype(F32), other[:, 0:width].astype(F32))
+        out[:, at : at + width] = value
+        at += width
+
+
+def join_rows(core, pairs, width):
+    rows = pairs[0][0].shape[0]
+    block = 48
+    steps = rows // block
+    specs, args = [], []
+    for pair in pairs:
+        for value in pair:
+            specs.append(pl.BlockSpec((block, value.shape[1]), lambda i, c: (i % steps, 0)))
+            args.append(value)
+    return pl.pallas_call(
+        partial(join_kernel, steps),
+        grid_spec=pltpu.PrefetchScalarGridSpec(
+            num_scalar_prefetch=1,
+            grid=(2 * steps,),
+            in_specs=specs,
+            out_specs=pl.BlockSpec((block, width), lambda i, c: (i, 0)),
+        ),
+        out_shape=jax.ShapeDtypeStruct((2 * rows, width), F32),
+        cost_estimate=pl.CostEstimate(
+            flops=1_000_000, bytes_accessed=20_000_000, transcendentals=0
+        ),
+        name="join_rows",
+    )(core.reshape(1), *args)
+
+
+def join_cols_kernel(core_ref, mine, other, out):
+    half = mine.shape[1]
+    first = core_ref[0] == 0
+    a, b = mine[...].astype(F32), other[...].astype(F32)
+    out[:, 0:half] = jnp.where(first, a, b)
+    out[:, half:] = jnp.where(first, b, a)
+
+
+def join_cols(core, mine, other):
+    rows, half = mine.shape
+    block = 128
+    spec = pl.BlockSpec((block, half), lambda i, c: (i, 0))
+    return pl.pallas_call(
+        join_cols_kernel,
+        grid_spec=pltpu.PrefetchScalarGridSpec(
+            num_scalar_prefetch=1,
+            grid=(rows // block,),
+            in_specs=[spec, spec],
+            out_specs=pl.BlockSpec((block, 2 * half), lambda i, c: (i, 0)),
+        ),
+        out_shape=jax.ShapeDtypeStruct((rows, 2 * half), F32),
+        cost_estimate=pl.CostEstimate(
+            flops=1_000_000, bytes_accessed=8_000_000, transcendentals=0
+        ),
+        name="join_cols",
+    )(core.reshape(1), mine, other)
 
 
 def make_masks(seg_ids, taps, head_count, inner):
@@ -618,17 +717,32 @@
     }
 
 
+TN = ((0,), (0,))
+
+
 def swap(value):
     return lax.ppermute(value, "core", [(0, 1), (1, 0)])
 
 
-def all_sum(value, axes):
-    for axis, size in axes:
-        step = 1
-        while step < size:
-            value = value + lax.ppermute(value, axis, [(i, i ^ step) for i in range(size)])
-            step *= 2
+def to_partner(value, axis, size, step):
+    return lax.ppermute(value, axis, [(i, i ^ step) for i in range(size)])
+
+
+def after(value, *others):
+    return lax.optimization_barrier((value,) + others)[0]
+
+
+def line_sum(value, size):
+    step = 1
+    while step < size:
+        moved = to_partner(value, "line", size, step)
+        value = (value.astype(F32) + moved.astype(F32)).astype(value.dtype)
+        step *= 2
     return value
+
+
+def pick(value, index, axis=0):
+    return lax.dynamic_index_in_dim(value, index, axis, keepdims=False)
 
 
 def local(
@@ -648,41 +762,63 @@
 ):
     line_n, core_n, shard_n = sizes
     core = lax.axis_index("core")
-    rows, width = hidden_in.shape
+    shard = lax.axis_index("shard")
+    _, width = hidden_in.shape
     inner = gate_gain.shape[0]
     heads = dt_bias.shape[0]
     taps, xbc = conv_weight.shape
     state_dim = (xbc - inner) // 2
-    shard_rows = in_weight.shape[0]
-    half = shard_rows // 2
+    half = in_weight.shape[0] // 2
+    quarter = half // 2
+    out_half = width // 2
     f_rest = in_weight.shape[1] - inner
     f_pad = -f_rest % 128
-
-    def split_cols(value):
+    f_wide = f_rest + f_pad
+
+    def split_rows(value):
         parts = value.reshape(value.shape[0], shard_n, 2, half)
-        mine = lax.dynamic_index_in_dim(parts, core, 2, keepdims=False)
-        other = lax.dynamic_index_in_dim(parts, 1 - core, 2, keepdims=False)
         flat = (value.shape[0], shard_n * half)
-        return mine.reshape(flat), other.reshape(flat)
-
-    def by_core(mine, other):
+        return pick(parts, core, 2).reshape(flat), pick(parts, 1 - core, 2).reshape(flat)
+
+    def join_split(mine, other):
+        shape = (mine.shape[0], shard_n, half)
+        mine, other = mine.reshape(shape), other.reshape(shape)
         first = jnp.where(core == 0, mine, other)
         second = jnp.where(core == 0, other, mine)
-        return first, second
-
-    def join_cols(mine, other):
-        shape = (mine.shape[0], shard_n, half)
-        first, second = by_core(mine.reshape(shape), other.reshape(shape))
         return jnp.stack([first, second], axis=2).reshape(mine.shape[0], width)
 
-    own_rows = lax.dynamic_slice_in_dim(in_weight, core * half, half, 0)
-    w1_own = jnp.pad(own_rows[:, inner:], ((0, 0), (0, f_pad)))
-    w1_m = lax.all_gather(w1_own, "shard", axis=0, tiled=True)
-    w1_o = swap(w1_m)
-    w0_m = lax.all_gather(own_rows[:, :inner], "shard", axis=0, tiled=True)
+    def halves(value):
+        parts = value.reshape(value.shape[0], 2, out_half)
+        return pick(parts, core, 1), pick(parts, 1 - core, 1)
+
+    own = jnp.pad(in_weight[:, inner:], ((0, 0), (0, f_pad)))
+    piece = pick(own.reshape(2, half, f_wide), core)
+    from_x = to_partner(piece, "shard", shard_n, 1)
+    from_y = to_partner(piece, "shard", shard_n, 2)
+    far_a = to_partner(from_y[:quarter], "shard", shard_n, 1)
+    far_b = to_partner(from_x[quarter:], "shard", shard_n, 2)
+    w1 = jnp.zeros((4 * shard_n, quarter, f_wide), BF16)
+
+    def put(whole, value, owner, which, part=0):
+        value = value.reshape(-1, quarter, f_wide)
+        return lax.dynamic_update_slice_in_dim(whole, value, owner * 4 + which * 2 + part, 0)
+
+    w1 = put(w1, own, shard, 0)
+    w1 = put(w1, from_x, shard ^ 1, core)
+    w1 = put(w1, from_y, shard ^ 2, core)
+    w1 = put(w1, swap(from_x), shard ^ 1, 1 - core)
+    w1 = put(w1, swap(from_y), shard ^ 2, 1 - core)
+    w1 = put(w1, far_a, shard ^ 3, core)
+    w1 = put(w1, far_b, shard ^ 3, core, 1)
+    w1 = put(w1, swap(far_a), shard ^ 3, 1 - core)
+    w1 = put(w1, swap(far_b), shard ^ 3, 1 - core, 1)
+    w1 = w1.reshape(width, f_wide)
+
+    own0 = pick(in_weight.reshape(2, half, -1)[:, :, :inner], core)
+    w0_m = lax.all_gather(own0, "shard", axis=0, tiled=True)
     w0_o = swap(w0_m)
-    wo_own, _ = split_cols(out_weight)
-    wo_m = lax.all_gather(wo_own, "shard", axis=0, tiled=True)
+    own_out, _ = halves(out_weight)
+    wo_m = lax.all_gather(own_out, "shard", axis=0, tiled=True)
     wo_o = swap(wo_m)
 
     masks = make_masks(seg_ids, taps, heads, inner)
@@ -690,95 +826,107 @@
     dt_bias_p, a_log_p = pad_heads(dt_bias), pad_heads(a_log)
     skip_wide = jnp.repeat(skip_gain, HD)[None]
 
-    hid_m, hid_o = split_cols(hidden_in)
-    cot_m, cot_o = split_cols(cotangent)
-    gain_m, gain_o = split_cols(norm_gain[None])
-    h_m, h_o = hid_m.astype(F32), hid_o.astype(F32)
-    square = jnp.sum(h_m * h_m, axis=-1, keepdims=True) + jnp.sum(h_o * h_o, axis=-1, keepdims=True)
-    r = lax.rsqrt(square * (1.0 / width) + EPS)
-    n_m = (h_m * r * gain_m).astype(BF16)
-    n_o = (h_o * r * gain_o).astype(BF16)
-
-    proj1 = (dot(n_m, w1_m) + dot(n_o, w1_o)).astype(BF16)
+    cot_m, cot_o = halves(cotangent)
+    hidden = hidden_in.astype(F32)
+    r = lax.rsqrt(jnp.mean(hidden * hidden, axis=-1, keepdims=True) + EPS)
+    normed = (hidden * r * norm_gain).astype(BF16)
+    n_m, n_o = split_rows(normed)
+
+    proj1 = dot(normed, w1).astype(BF16)
     saved = run_forward(
         proj1, inner, heads, state_dim, conv_weight, conv_bias[None], dt_bias_p, a_log_p,
         skip_wide, masks,
     )
-    gate = (dot(n_m, w0_m) + dot(n_o, w0_o)).astype(BF16)
-    d_mixer = (dot(cot_m, wo_m, NT) + dot(cot_o, wo_o, NT)).astype(BF16)
-    mixer_out, d_y, d_gate, gg = run_norm(saved[2], gate, d_mixer, gate_gain[None], masks["live"])
-
-    tn = ((0,), (0,))
+    n_m2, n_o2 = lax.optimization_barrier((n_m, n_o, saved[2]))[:2]
+    gate = (dot(n_m2, w0_m) + dot(n_o2, w0_o)).astype(BF16)
+    cot_m2, cot_o2 = lax.optimization_barrier((cot_m, cot_o, gate))[:2]
+    d_mixer = (dot(cot_m2, wo_m, NT) + dot(cot_o2, wo_o, NT)).astype(BF16)
+    mixer_out, d_y, d_gate, gg = run_norm(
+        saved[2], gate, d_mixer, gate_gain[None], masks["live"], taps
+    )
 
     def reduce_pair(lhs_m, lhs_o, rhs_m, rhs_o):
-        sent = swap(dot(lhs_o, rhs_o, tn).astype(BF16))
-        return (dot(lhs_m, rhs_m, tn) + sent.astype(F32)).astype(BF16)
-
-    def reduce_rest(value):
-        part = lax.psum_scatter(value, "shard", scatter_dimension=0, tiled=True)
-        return lax.psum(part, "line")
-
-    g0 = reduce_rest(reduce_pair(n_m, n_o, d_gate, d_gate))
-    go = reduce_rest(reduce_pair(mixer_out, mixer_out, cot_m, cot_o))
-
-    d_x, x_sums, d_bc, bc_sums, d_dt, small = run_backward(
-        d_y, saved, proj1, heads, state_dim, conv_weight, dt_bias_p, a_log_p, skip_wide, masks
-    )
-    d_proj1 = jnp.concatenate([d_x, d_bc, d_dt], axis=1)
-    g1 = reduce_rest(reduce_pair(n_m, n_o, d_proj1, d_proj1))
+        sent = swap(dot(lhs_o, rhs_o, TN).astype(BF16))
+        return (dot(lhs_m, rhs_m, TN) + sent.astype(F32)).astype(BF16)
+
+    def scatter(value):
+        return lax.psum_scatter(value, "shard", scatter_dimension=0, tiled=True)
+
+    go_pair = reduce_pair(mixer_out, mixer_out, cot_m, cot_o)
+    go = scatter(go_pair)
+    g0_pair = reduce_pair(n_m, n_o, after(d_gate, go_pair), d_gate)
+    g0 = scatter(g0_pair)
+
+    groups = inner // (HEADS_STEP * HD)
+    cut = (2 * groups) // 3
+    first = run_backward(
+        after(d_y, g0_pair), saved, proj1, heads, state_dim, conv_weight, dt_bias_p, a_log_p,
+        skip_wide, masks, (0, cut),
+    )
+    d_xa, sums_a, kept = first[0], first[1], first[2:]
+    ga_pair = reduce_pair(n_m, n_o, d_xa, d_xa)
+    ga = scatter(ga_pair)
+    d_xb, sums_b, d_bc, sums_bc, d_dt, small = run_backward(
+        d_y, saved, proj1, heads, state_dim, conv_weight, dt_bias_p, a_log_p, skip_wide,
+        masks, (cut, groups), kept,
+    )
+    d_last = jnp.concatenate([d_xb, d_bc, d_dt], axis=1)
+    gb_pair = reduce_pair(n_m, n_o, d_last, d_last)
+
+    ypos, xpos = shard // 2, shard % 2
+    blocks = gb_pair.reshape(2, 2, half, -1)
+    add = lambda a, b: (a.astype(F32) + b.astype(F32)).astype(BF16)
+    upper, lower = blocks[:, :, :quarter], blocks[:, :, quarter:]
+    up = add(pick(upper, xpos, 1), to_partner(pick(upper, 1 - xpos, 1), "shard", shard_n, 1))
+    lo = add(pick(lower, ypos, 0), to_partner(pick(lower, 1 - ypos, 0), "shard", shard_n, 2))
+    up = add(pick(up, ypos), to_partner(pick(up, 1 - ypos), "shard", shard_n, 2))
+    lo = add(pick(lo, xpos), to_partner(pick(lo, 1 - xpos), "shard", shard_n, 1))
+    gb = line_sum(jnp.concatenate([up, lo], axis=0), line_n)
+    go, g0, ga = line_sum(go, line_n), line_sum(g0, line_n), line_sum(ga, line_n)
 
     branch_m, branch_o = dot(mixer_out, wo_m), dot(mixer_out, wo_o)
-    block_out = join_cols((h_m + branch_m).astype(BF16), (h_o + branch_o).astype(BF16))
-
-    dn_m = dot(d_gate, w0_m, NT) + dot(d_proj1, w1_m, NT)
-    dn_o = dot(d_gate, w0_o, NT) + dot(d_proj1, w1_o, NT)
-    ng = join_cols(
-        jnp.sum(dn_m * h_m * r, axis=0, keepdims=True), jnp.sum(dn_o * h_o * r, axis=0, keepdims=True)
-    )[0]
-    gd_m, gd_o = gain_m * dn_m, gain_o * dn_o
-    mean = (
-        jnp.sum(h_m * gd_m, axis=-1, keepdims=True) + jnp.sum(h_o * gd_o, axis=-1, keepdims=True)
-    ) * (1.0 / width)
-    back = r * r * r * mean
-    input_grad = join_cols(
-        cot_m.astype(F32) + r * gd_m - h_m * back, cot_o.astype(F32) + r * gd_o - h_o * back
-    )
-
-    sums = jnp.concatenate([x_sums.sum(1), bc_sums.sum(1)], axis=1)
-    per_head = small.sum(1)
-    packed = jnp.concatenate([sums.reshape(-1), per_head.reshape(-1), gg.sum(0), ng])
-    packed = jnp.pad(packed, (0, -packed.shape[0] % 1024)).reshape(-1, 128)
-    packed = all_sum(packed, (("core", core_n), ("shard", shard_n), ("line", line_n))).reshape(-1)
-    sums = packed[: (taps + 1) * xbc].reshape(taps + 1, xbc)
-    at = (taps + 1) * xbc
-    per_head = packed[at : at + 384].reshape(3, 128)[:, :heads]
-    at += 384
-    gate_gain_grad = packed[at : at + inner]
-    norm_gain_grad = packed[at + inner : at + inner + width]
-
-    g0_first, g0_second = by_core(g0, swap(g0))
-    g1_first, g1_second = by_core(g1[:, :f_rest], swap(g1)[:, :f_rest])
-    in_grad = jnp.concatenate(
-        [
-            jnp.concatenate([g0_first, g1_first], axis=1),
-            jnp.concatenate([g0_second, g1_second], axis=1),
-        ],
-        axis=0,
-    ).astype(F32)
-    out_grad = join_cols(go, swap(go)).astype(F32)
-    return (
+    block_out = (hidden + join_cols(core, branch_m, branch_o)).astype(BF16)
+
+    d_proj1 = jnp.concatenate([d_xa, d_last], axis=1)
+    dn = dot(d_proj1, w1, NT) + join_split(dot(d_gate, w0_m, NT), dot(d_gate, w0_o, NT))
+    ng = jnp.sum(dn * (hidden * r), axis=0, keepdims=True)
+    gd = norm_gain * dn
+    mean = jnp.mean(hidden * gd, axis=-1, keepdims=True)
+    input_grad = cotangent.astype(F32) + r * gd - hidden * (r * r * r * mean)
+
+    packed = jnp.concatenate(
+        [jnp.concatenate([sums_a, sums_b], axis=1) + gg, sums_bc], axis=1
+    )
+    tail = jnp.concatenate([ng, small[0:1], small[1:2], small[2:3]], axis=1)
+    tail = jnp.pad(tail, ((taps + 2, 8 - taps - 3), (0, xbc - tail.shape[1])))
+    packed = packed + tail
+    for axis, size in (("core", core_n), ("shard", shard_n), ("line", line_n)):
+        packed = line_sum_on(packed, axis, size)
+    last = packed[taps + 2]
+
+    outs = (
         block_out,
         input_grad,
-        norm_gain_grad,
-        in_grad,
-        sums[1:][::-1],
-        sums[0],
-        per_head[0],
-        per_head[1],
-        per_head[2],
-        gate_gain_grad,
-        out_grad,
-    )
+        last[:width],
+        packed[:taps],
+        packed[taps],
+        last[width : width + heads],
+        last[width + 128 : width + 128 + heads],
+        last[width + 256 : width + 256 + heads],
+        packed[taps + 1, :inner],
+        join_cols(core, go, swap(go)),
+    )
+    pairs = [(g0, swap(g0)), (ga, swap(ga)), (gb, swap(gb))]
+    in_grad = join_rows(core, pairs, inner + f_rest)
+    return outs[:3] + (in_grad,) + outs[3:]
+
+
+def line_sum_on(value, axis, size):
+    step = 1
+    while step < size:
+        value = value + to_partner(value, axis, size, step)
+        step *= 2
+    return value
 
 
 def solution(mesh):

time: 697 us -> 678 us (0.973)
  waiting for transfers between devices: 360 us -> 287 us
  Pallas kernels: 80.8 us -> 108 us
  starting transfers between devices: 8.67 us -> 33.2 us
  other arithmetic: 51.6 us -> 32.2 us
  matrix products: 91.8 us -> 105 us
  local copies, waits for them, and re-layouts: 81.9 us -> 89.9 us
    ppermute x5 -> x21, waiting for transfers between devices: 3.32 us -> 206 us  [to_partner(): return lax.ppermute(value, axis, [(i, i ^ step) for i in range(size)])]
    psum x1 -> x0, waiting for transfers between devices: 112 us -> none  [reduce_rest(): return lax.psum(part, 'line')]
    all_gather x3 -> x2, waiting for transfers between devices: 150 us -> 47.8 us  [the longest x1 47.8 us: local(): wo_m = lax.all_gather(own_out, 'shard', axis=0, tiled=True)]
    reduce_scatter x3, waiting for transfers between devices: 76.5 us -> 26.3 us  [scatter(): return lax.psum_scatter(value, 'shard', scatter_dimension=0, tiled=True)]
    pallas_call x2 -> x6, Pallas kernels: 55.8 us -> 82.5 us  [the longest x2 50.2 us: run_backward(): pl.pallas_call(partial(backward_kernel, head_count, first, opens, closes)...]
    ppermute x5 -> x21, starting transfers between devices: 5.88 us -> 30.8 us  [to_partner(): return lax.ppermute(value, axis, [(i, i ^ step) for i in range(size)])]
    convert_element_type x4 -> x13, other arithmetic: 24.1 us -> 9.24 us  [the longest x8 5.84 us: line_sum(): value = (value.astype(F32) + moved.astype(F32)).astype(value.dtype)]
    dynamic_update_slice x0 -> x9, local copies, waits for them, and re-layouts: none -> 13.9 us  [put(): lax.dynamic_update_slice_in_dim(whole, value, owner * 4 + which * 2 + par...]
  transfers between devices with their start and end apart: 21 -> 40, of which waited for: 10 -> 16; matrix products, arithmetic and copies ran while one was open for 25% -> 27% of each run, Pallas kernels for 6% -> 9%
where the time goes in v2:
time: 678 us; the launch traced here: 670 us
  waiting for transfers between devices  287 us (42%)
  Pallas kernels  108 us (16%)
  matrix products  105 us (15%)
  local copies, waits for them, and re-layouts  89.9 us (13%)
  starting transfers between devices  33.2 us (5%)
  other arithmetic  32.2 us (5%)
  between operations  15 us (2%)
    ppermute x21, waiting for transfers between devices, to_partner(): return lax.ppermute(value, axis, [(i, i ^ step) for i in range(size)])  206 us
    dot_general x18, matrix products, dot(): lax.dot_general(a, b, (dims, ((), ())), preferred_element_type=F32, preci...  105 us
    pallas_call x2, Pallas kernels, run_backward(): pl.pallas_call(partial(backward_kernel, head_count, first, opens, closes)...  50.2 us
    all_gather x1, waiting for transfers between devices, local(): wo_m = lax.all_gather(own_out, 'shard', axis=0, tiled=True)  47.8 us
    unnamed x128, local copies, waits for them, and re-layouts  35.9 us
    ppermute x21, starting transfers between devices, to_partner(): return lax.ppermute(value, axis, [(i, i ^ step) for i in range(size)])  30.8 us
    reduce_scatter x3, waiting for transfers between devices, scatter(): return lax.psum_scatter(value, 'shard', scatter_dimension=0, tiled=True)  26.3 us
    pallas_call x1, Pallas kernels, run_forward(): pl.pallas_call(partial(forward_kernel, head_count), grid=(groups,), in_sp...  25.1 us
  transfers between devices with their start and end apart: 40, of which 16 were waited for; matrix products, arithmetic and copies ran while one was open for 27% of the time, Pallas kernels for 9%

profile of v2, /device:TPU:8, one launch (start us, length us, event | category | flops | bytes accessed | tf_op | source)
XLA Modules:
  0.0 669.9 jit_solution(10817664575092595213)
XLA Ops:
  7.2 7.5 %copy.52 = bf16[384,6448]{1,0:T(8,128)(2,1)} copy(bf16[384,6448]{0,1:T(8,128)(2,1)} %param.15) | data formatting | bytes 9904128 | tf_op args[3]
  24.1 4.3 copy.58
  37.4 3.0 fusion.18
  40.4 2.7 copy.53
  50.5 4.0 copy-done.2
  60.1 7.6 %collective-permute-done = bf16[192,3456]{1,0:T(8,128)(2,1)} collective-permute-done((bf16[192,3456]{1,0:T(8,128)(2,1)}, bf16[192,3456]{1,0:T(8,128)(2,1)}, u32[]{:S(2)}, u32[]{:S(2)}) %collective-permute-start) | collective-permute-done | bytes 1327136 | tf_op jit(solution)/shard_map/ppermute | solution.py:728
  83.9 20.4 %collective-permute-done.4 = bf16[96,3456]{1,0:T(8,128)(2,1)S(1)} collective-permute-done((bf16[96,3456]{1,0:T(8,128)(2,1)S(1)}, bf16[96,3456]{1,0:T(8,128)(2,1)S(1)}, u32[]{:S(2)}, u32[]{:S(2)}) %collective-permute-start.4) | collective-permute-done | bytes 663584 | tf_op jit(solution)/shard_map/ppermute | solution.py:728
  114.5 47.8 %all-gather.7.cloned.1.call-done = bf16[3072,1,768]{0,2,1:T(8,128)(2,1)} async-done(((bf16[768,1,768]{0,2,1:T(8,128)(2,1)}), bf16[3072,1,768]{0,2,1:T(8,128)(2,1)}) %all-gather.7.cloned.1.call-update) | async-done | bytes 4718608 | tf_op jit(solution)/shard_map/all_gather | solution.py:821
  162.3 6.6 copy.59
  168.9 11.3 %convolution_convert_fusion.x_in.bc_in.dt_in = bf16[512,3456]{1,0:T(8,128)(2,1)} fusion(bf16[512,1536]{1,0:T(8,128)(2,1)S(1)} %copy-done.5, bf16[1536,3456]{1,0:T(8,128)(2,1)} %bitcast.140), kind=kOutput, calls=%fused_computation.12 | convolution fusion | flops 5437587456 | bytes 15728640 | tf_op jit(solution)/shard_map/dot_general | solution.py:21
  180.2 25.1 %scan_forward.1 = (bf16[512,3072]{1,0:T(8,128)(2,1)}, bf16[512,3072]{1,0:T(8,128)(2,1)}, bf16[512,3072]{1,0:T(8,128)(2,1)}, bf16[4,128,3072]{2,1,0:T(8,128)(2,1)...) custom-call(bf16[512,3456]{1,0:T(8,128)(2,1)} %convolution_convert_f, ...), custom_call_target="tpu_custom_call" | custom-call | flops 20000000000 | bytes 20000000 | tf_op jit(solution)/shard_map/scan_forward/pallas_call | solution.py:176
  205.3 4.7 fusion.56
  210.0 6.8 %add_convert_fusion.4.z_ref = bf16[512,3072]{1,0:T(8,128)(2,1)} fusion(f32[512,3072]{1,0:T(8,128)S(1)} %fusion.56, bf16[512,768]{0,1:T(8,128)(2,1)S(1)} %bitcast.149, bf16[768,3072]{1,0:T(8,128)(2,1)} %collective-permute-done.8), kind=kOutput, calls=%fused_computation.4 | convolution fusion | flops 2419064832 | bytes 14942208 | tf_op jit(solution)/shard_map/dot_general | solution.py:21
  216.8 2.7 fusion.3
  219.5 6.3 add_convert_fusion.3.dm_ref
  226.7 12.6 %gated_norm.1 = (bf16[512,3072]{1,0:T(8,128)(2,1)}, bf16[512,3072]{1,0:T(8,128)(2,1)}, bf16[512,3072]{1,0:T(8,128)(2,1)}, f32[8,3072]{1,0:T(8,128)}) custom-call(bf16[512,3072]{1,0:T(8,128)(2,1)} %get-tuple-element.45.y_ref, bf16[512,3072]{1,0:T(8,128)(2,1)} %add_convert_fusion.4.z_ref, bf16[512,3072]{1,0:T(8,128)(2,1)} %add_convert_fusion.3.dm_ref, ...), custom_call_target="tpu_custom_call" | custom-call | flops 10000000000 | bytes 20000000 | tf_op jit(solution)/shard_map/gated_norm/pallas_call | solution.py:279
  239.3 4.7 convolution_convert_fusion.2
  244.6 4.2 convolution_convert_fusion.1
  250.3 3.6 fusion.25.hs
  253.8 4.8 add_convert_fusion.1
  259.0 6.8 %add_convert_fusion = bf16[768,3072]{1,0:T(8,128)(2,1)} fusion(bf16[768,3072]{1,0:T(8,128)(2,1)} %collective-permute-done.11, bf16[512,768]{0,1:T(8,128)(2,1)S(1)} %bitcast.155, bf16[512,3072]{1,0:T(8,128)(2,1)} %get-tuple-element.53), kind=kOutput, calls=%fused_computation | convolution fusion | flops 2422996992 | bytes 13369344 | tf_op jit(solution)/shard_map/dot_general | solution.py:21
  265.8 30.7 %scan_backward.2 = (bf16[512,2048]{1,0:T(8,128)(2,1)}, f32[8,2048]{1,0:T(8,128)}, f32[512,128]{1,0:T(8,128)}, f32[512,128]{1,0:T(8,128)}, f32[512,128]{1,0:T(8,1...) custom-call(bf16[512,3072]{1,0:T(8,128)(2,1)} %get-tuple-element.54.dy_ref, ...), custom_call_target="tpu_custom_call" | custom-call | flops 26666665984 | bytes 13333333 | tf_op jit(solution)/shard_map/scan_backward/pallas_call | solution.py:556
  296.5 3.5 convolution_convert_fusion.3
  300.5 5.3 collective-permute-done.20
  305.8 3.4 add_convert_fusion.2
  311.2 5.1 fusion.54
  316.3 6.2 broadcast_select_fusion.1
  327.9 19.5 %scan_backward.3 = (bf16[512,1024]{1,0:T(8,128)(2,1)}, f32[8,1024]{1,0:T(8,128)}, bf16[512,256]{1,0:T(8,128)(2,1)}, f32[8,256]{1,0:T(8,128)}, bf16[512,128]{1,0:T(8,128)(2,1)}, /*index=5*/f32[8,128]{1,0:T(8,128)}) custom-call(bf16[512,3072]{1,0:T(8,128)(2,1)} %get-tuple-element.54.dy_ref, bf16[512,3072]{1,0:T(8,128)(2,1)} %get-tuple-element.55.x_ref, ...), custom_call_target="tpu_custom_call" | custom-call | flops 13333332992 | bytes 6666666 | tf_op jit(solution)/shard_map/scan_backward/pallas_call | solution.py:556
  351.3 4.4 convolution_convert_fusion.4
  356.0 13.3 %fusion.19 = (f32[1536]{0:T(1024)S(1)}, f32[512]{0:T(512)}, f32[512,1536]{1,0:T(8,128)}) fusion(bf16[512,1536]{1,0:T(8,128)(2,1)S(1)} %copy-done, f32[512]{0:T(512)S(1)} %copy-done.35, f32[1536]{0:T(1024)S(1)} %copy-done.28, f32[512,1536]{1,0:T(8,128)S(1)} %copy-done.11, bf16[1536,3456]{1,0:T(8,128)(2,1)} %bitcast.141, bf16[512,128]{1,0:T(8,128)(2,1)S(1)} %copy-done.26, ...), kind=kOutput, calls=%fused_computation.34 | convolution fusion | flops 5456263168 | bytes 22036480 | tf_op jit(solution)/shard_map/dot_general | solution.py:21
  374.1 3.4 add_convert_fusion.5
  379.4 6.2 fusion.1.mine
  387.8 14.8 %collective-permute-done.27 = bf16[2,96,1408]{2,1,0:T(8,128)(2,1)S(1)} collective-permute-done((bf16[2,96,1408]{2,1,0:T(8,128)(2,1)S(1)}, bf16[2,96,1408]{2,1,0:T(8,128)(2,1)S(1)}, u32[]{:S(2)}, u32[]{:S(2)}) %collective-permute-start.27) | collective-permute-done | bytes 540704 | tf_op jit(solution)/shard_map/ppermute | solution.py:728
  406.5 4.9 collective-permute-done.28
  411.5 5.0 collective-permute-done.26
  418.8 7.4 %fusion.60.other = f32[512,768]{1,0:T(8,128)} fusion(bf16[512,3072]{1,0:T(8,128)(2,1)} %get-tuple-element.50, bf16[3072,768]{1,0:T(8,128)(2,1)} %collective-permute-done.9), kind=kOutput, calls=%fused_computation.170 | convolution fusion | flops 2415919104 | bytes 9437184 | tf_op jit(solution)/shard_map/dot_general | solution.py:21
  426.2 4.2 join_cols.2
  432.6 23.7 %collective-permute-done.15 = f32[8,3328]{1,0:T(8,128)S(1)} collective-permute-done((f32[8,3328]{1,0:T(8,128)S(1)}, f32[8,3328]{1,0:T(8,128)S(1)}, u32[]{:S(2)}, u32[]{:S(2)}) %collective-permute-start.15) | collective-permute-done | bytes 106528 | tf_op jit(solution)/shard_map/ppermute | solution.py:728
  457.0 4.1 collective-permute-start.16
  461.3 26.3 %reduce-scatter.8.cloned.1.call-done = bf16[768,768]{1,0:T(8,128)(2,1)} async-done(((bf16[3072,768]{1,0:T(8,128)(2,1)}), bf16[768,768]{1,0:T(8,128)(2,1)}) %reduce-scatter.8.cloned.1.call-update) | async-done | bytes 1179664 | tf_op jit(solution)/shard_map/reduce_scatter | solution.py:853
  494.7 42.3 %collective-permute-done.32 = bf16[768,768]{1,0:T(8,128)(2,1)S(1)} collective-permute-done((bf16[768,768]{1,0:T(8,128)(2,1)}, bf16[768,768]{1,0:T(8,128)(2,1)S(1)}, u32[]{:S(2)}, u32[]{:S(2)}) %collective-permute-start.32) | collective-permute-done | bytes 1179680 | tf_op jit(solution)/shard_map/ppermute | solution.py:728
  537.3 3.3 collective-permute-start.33
  541.0 61.8 %collective-permute-done.18 = bf16[192,3072]{1,0:T(8,128)(2,1)S(1)} collective-permute-done((bf16[192,3072]{1,0:T(8,128)(2,1)S(1)}, bf16[192,3072]{1,0:T(8,128)(2,1)S(1)}, u32[]{:S(2)}, u32[]{:S(2)}) %collective-permute-start.18) | collective-permute-done | bytes 1179680 | tf_op jit(solution)/shard_map/ppermute | solution.py:728
  603.4 23.3 %collective-permute-done.33 = bf16[768,768]{1,0:T(8,128)(2,1)S(1)} collective-permute-done((bf16[768,768]{1,0:T(8,128)(2,1)S(1)}, bf16[768,768]{1,0:T(8,128)(2,1)S(1)}, u32[]{:S(2)}, u32[]{:S(2)}) %collective-permute-start.33) | collective-permute-done | bytes 1179680 | tf_op jit(solution)/shard_map/ppermute | solution.py:728
  628.1 3.1 fusion.23
  636.9 9.9 %join_rows.1 = f32[384,6448]{1,0:T(8,128)} custom-call(s32[1]{0:T(128)} %bitcast.core_ref, bf16[192,3072]{1,0:T(8,128)(2,1)} %copy-done.6, bf16[192,3072]{1,0:T(8,128)(2,1)} %collective-permute-done.19.refs_1_, bf16[192,2048]{1,0:T(8,128)(2,1)} %copy-done.9, bf16[192,2048]{1,0:T(8,128)(2,1)} %copy-done.22, bf16[192,1408]{1,0:T(8,128)(2,1)} %copy-done.18, ...), custom_call_target="tpu_custom_call" | custom-call | flops 1000000 | bytes 20000000 | tf_op jit(solution)/shard_map/join_rows/pallas_call | solution.py:618
  646.9 10.7 %copy.64 = f32[384,6448]{0,1:T(8,128)} copy(f32[384,6448]{1,0:T(8,128)} %join_rows.1) | data formatting | bytes 19808256
  657.5 5.6 join_cols.3
  (298 shorter events, 105.9 us)
Async XLA Ops:
  7.2 104.8 %all-gather.5.cloned.1.call-start = ((), (), s32[]{:S(2)}) async-start(), calls=%async_computation.6 | async-start | bytes 5898240 | tf_op jit(solution)/shard_map/all_gather | solution.py:818
  17.7 144.5 %all-gather.7.cloned.1.call-start = ((), (), s32[]{:S(2)}) async-start(), calls=%async_computation.7 | async-start | bytes 5898240 | tf_op jit(solution)/shard_map/all_gather | solution.py:821
  21.1 46.5 %collective-permute-start = (bf16[192,3456]{1,0:T(8,128)(2,1)}, bf16[192,3456]{1,0:T(8,128)(2,1)}, u32[]{:S(2)}, u32[]{:S(2)}) collective-permute-start(bf16[192,3456]{1,0:T(8,128)(2,1)} %dynamic-slice_bitcast_fusion), channel_id=1, source_target_pairs={{0,1},{1,0},{2,3},{3,2},{4,5},{5,4},{6,7},{7,6},{8,9},{9,8},{10,11... | collective-permute-start | bytes 3981320 | tf_op jit(solution)/shard_map/ppermute | solution.py:728
  22.6 49.9 %collective-permute-start.1 = (bf16[192,3456]{1,0:T(8,128)(2,1)}, bf16[192,3456]{1,0:T(8,128)(2,1)}, u32[]{:S(2)}, u32[]{:S(2)}) collective-permute-start(bf16[192,3456]{1,0:T(8,128)(2,1)} %dynamic-slice_bitcast_fusion), channel_id=1, source_target_pairs={{0,2},{1,3},{2,0},{3,1},{4,6},{5,7},{6,4},{7,5},{8,10},{9,11},{10,... | collective-permute-start | bytes 3981320 | tf_op jit(solution)/shard_map/ppermute | solution.py:728
  31.1 386.5 %reduce-scatter.6.cloned.1.call-start = ((), (), s32[]{:S(2)}) async-start(), calls=%async_computation.4 | async-start | bytes 3932160 | tf_op jit(solution)/shard_map/reduce_scatter | solution.py:853
  49.3 247.2 %copy-start.7 = (bf16[512,4,1,192]{0,3,2,1:T(8,128)(2,1)}, bf16[512,4,1,192]{0,3,2,1:T(8,128)(2,1)S(1)}, u32[]{:S(2)}) copy-start(bf16[512,4,1,192]{0,3,2,1:T(8,128)(2,1)S(1)} %get-tuple-element.133) | copy-start | bytes 2359300
  67.6 37.9 %collective-permute-start.2 = (bf16[192,3456]{1,0:T(8,128)(2,1)}, bf16[192,3456]{1,0:T(8,128)(2,1)}, u32[]{:S(2)}, u32[]{:S(2)}) collective-permute-start(bf16[192,3456]{1,0:T(8,128)(2,1)} %collective-permute-done), channel_id=1, source_target_pairs={{0,4},{4,0},{1,5},{5,1},{2,6},{6,2},{3,7},{7,3},{8,12},{12,8},{9,1... | collective-permute-start | bytes 3981320 | tf_op jit(solution)/shard_map/ppermute | solution.py:724
  73.6 30.7 %collective-permute-start.4 = (bf16[96,3456]{1,0:T(8,128)(2,1)S(1)}, bf16[96,3456]{1,0:T(8,128)(2,1)S(1)}, u32[]{:S(2)}, u32[]{:S(2)}) collective-permute-start(bf16[96,3456]{1,0:T(8,128)(2,1)S(1)} %slice.126), channel_id=1, source_target_pairs={{0,1},{1,0},{2,3},{3,2},{4,5},{5,4},{6,7},{7,6},{8,9},{9,8},{10,11... | collective-permute-start | bytes 1990664 | tf_op jit(solution)/shard_map/ppermute | solution.py:728
  77.3 28.3 %collective-permute-start.5 = (bf16[96,3456]{1,0:T(8,128)(2,1)S(1)}, bf16[96,3456]{1,0:T(8,128)(2,1)S(1)}, u32[]{:S(2)}, u32[]{:S(2)}) collective-permute-start(bf16[96,3456]{1,0:T(8,128)(2,1)S(1)} %slice.127), channel_id=1, source_target_pairs={{0,2},{1,3},{2,0},{3,1},{4,6},{5,7},{6,4},{7,5},{8,10},{9,11},{10,... | collective-permute-start | bytes 1990664 | tf_op jit(solution)/shard_map/ppermute | solution.py:728
  78.9 29.2 %collective-permute-start.3 = (bf16[192,3456]{1,0:T(8,128)(2,1)}, bf16[192,3456]{1,0:T(8,128)(2,1)S(1)}, u32[]{:S(2)}, u32[]{:S(2)}) collective-permute-start(bf16[192,3456]{1,0:T(8,128)(2,1)} %collective-permute-done.1), channel_id=1, source_target_pairs={{0,4},{4,0},{1,5},{5,1},{2,6},{6,2},{3,7},{7,3},{8,12},{12,8},{9,1... | collective-permute-start | bytes 3981320 | tf_op jit(solution)/shard_map/ppermute | solution.py:724
  104.3 6.8 %collective-permute-start.6 = (bf16[96,3456]{1,0:T(8,128)(2,1)S(1)}, bf16[96,3456]{1,0:T(8,128)(2,1)S(1)}, u32[]{:S(2)}, u32[]{:S(2)}) collective-permute-start(bf16[96,3456]{1,0:T(8,128)(2,1)S(1)} %collective-permute-done.4), channel_id=1, source_target_pairs={{0,4},{4,0},{1,5},{5,1},{2,6},{6,2},{3,7},{7,3},{8,12},{12,8},{9,1... | collective-permute-start | bytes 1990664 | tf_op jit(solution)/shard_map/ppermute | solution.py:724
  105.5 6.9 %collective-permute-start.7 = (bf16[96,3456]{1,0:T(8,128)(2,1)S(1)}, bf16[96,3456]{1,0:T(8,128)(2,1)}, u32[]{:S(2)}, u32[]{:S(2)}) collective-permute-start(bf16[96,3456]{1,0:T(8,128)(2,1)S(1)} %collective-permute-done.5), channel_id=1, source_target_pairs={{0,4},{4,0},{1,5},{5,1},{2,6},{6,2},{3,7},{7,3},{8,12},{12,8},{9,1... | collective-permute-start | bytes 1990664 | tf_op jit(solution)/shard_map/ppermute | solution.py:724
  112.0 98.0 %collective-permute-start.8 = (bf16[768,3072]{1,0:T(8,128)(2,1)}, bf16[768,3072]{1,0:T(8,128)(2,1)}, u32[]{:S(2)}, u32[]{:S(2)}) collective-permute-start(bf16[768,3072]{1,0:T(8,128)(2,1)} %bitcast.148), channel_id=1, source_target_pairs={{0,4},{4,0},{1,5},{5,1},{2,6},{6,2},{3,7},{7,3},{8,12},{12,8},{9,1... | collective-permute-start | bytes 14155784 | tf_op jit(solution)/shard_map/ppermute | solution.py:724
  114.5 54.4 %copy-start.5 = (bf16[512,1536]{1,0:T(8,128)(2,1)S(1)}, bf16[512,1536]{1,0:T(8,128)(2,1)}, u32[]{:S(2)}) copy-start(bf16[512,1536]{1,0:T(8,128)(2,1)} %fusion.18) | copy-start | bytes 4718596
  168.9 50.6 %collective-permute-start.9 = (bf16[3072,768]{1,0:T(8,128)(2,1)}, bf16[3072,768]{1,0:T(8,128)(2,1)}, u32[]{:S(2)}, u32[]{:S(2)}) collective-permute-start(bf16[3072,768]{1,0:T(8,128)(2,1)} %bitcast.147), channel_id=1, source_target_pairs={{0,4},{4,0},{1,5},{5,1},{2,6},{6,2},{3,7},{7,3},{8,12},{12,8},{9,1... | collective-permute-start | bytes 14155784 | tf_op jit(solution)/shard_map/ppermute | solution.py:724
  244.0 9.8 %collective-permute-start.10 = (bf16[3072,768]{1,0:T(8,128)(2,1)S(1)}, bf16[3072,768]{1,0:T(8,128)(2,1)S(1)}, u32[]{:S(2)}, u32[]{:S(2)}) collective-permute-start(bf16[3072,768]{1,0:T(8,128)(2,1)S(1)} %convolution_convert_fusion.2), channel_id=1, source_target_pairs={{0,4},{4,0},{1,5},{5,1},{2,6},{6,2},{3,7},{7,3},{8,12},{12,8},{9,1... | collective-permute-start | bytes 14155784 | tf_op jit(solution)/shard_map/ppermute | solution.py:724
  248.8 10.2 %collective-permute-start.11 = (bf16[768,3072]{1,0:T(8,128)(2,1)}, bf16[768,3072]{1,0:T(8,128)(2,1)}, u32[]{:S(2)}, u32[]{:S(2)}) collective-permute-start(bf16[768,3072]{1,0:T(8,128)(2,1)} %convolution_convert_fusion.1), channel_id=1, source_target_pairs={{0,4},{4,0},{1,5},{5,1},{2,6},{6,2},{3,7},{7,3},{8,12},{12,8},{9,1... | collective-permute-start | bytes 14155784 | tf_op jit(solution)/shard_map/ppermute | solution.py:724
  300.1 5.7 collective-permute-start.20
  309.3 122.0 %reduce-scatter.4.cloned.1.call-start = ((), (), s32[]{:S(2)}) async-start(), calls=%async_computation.3 | async-start | bytes 5898240 | tf_op jit(solution)/shard_map/reduce_scatter | solution.py:853
  309.9 177.7 %reduce-scatter.8.cloned.1.call-start = ((), (), s32[]{:S(2)}) async-start(), calls=%async_computation.5 | async-start | bytes 5898240 | tf_op jit(solution)/shard_map/reduce_scatter | solution.py:853
  355.7 18.3 %collective-permute-start.24 = (bf16[768,1408]{1,0:T(8,128)(2,1)}, bf16[768,1408]{1,0:T(8,128)(2,1)}, u32[]{:S(2)}, u32[]{:S(2)}) collective-permute-start(bf16[768,1408]{1,0:T(8,128)(2,1)} %convolution_convert_fusion.4), channel_id=1, source_target_pairs={{0,4},{4,0},{1,5},{5,1},{2,6},{6,2},{3,7},{7,3},{8,12},{12,8},{9,1... | collective-permute-start | bytes 6488072 | tf_op jit(solution)/shard_map/ppermute | solution.py:724
  371.1 1.4 collective-permute-start.12
  372.5 13.1 %collective-permute-start.13 = (f32[8,3328]{1,0:T(8,128)S(1)}, f32[8,3328]{1,0:T(8,128)S(1)}, u32[]{:S(2)}, u32[]{:S(2)}) collective-permute-start(f32[8,3328]{1,0:T(8,128)S(1)} %add.260), channel_id=1, source_target_pairs={{0,1},{1,0},{2,3},{3,2},{4,5},{5,4},{6,7},{7,6},{8,9},{9,8},{10,11... | collective-permute-start | bytes 319496 | tf_op jit(solution)/shard_map/ppermute | solution.py:728
  377.7 24.8 %collective-permute-start.27 = (bf16[2,96,1408]{2,1,0:T(8,128)(2,1)S(1)}, bf16[2,96,1408]{2,1,0:T(8,128)(2,1)S(1)}, u32[]{:S(2)}, u32[]{:S(2)}) collective-permute-start(bf16[2,96,1408]{2,1,0:T(8,128)(2,1)S(1)} %dynamic-slice_bitcast_fusion.1), channel_id=1, source_target_pairs={{0,2},{1,3},{2,0},{3,1},{4,6},{5,7},{6,4},{7,5},{8,10},{9,11},{10,... | collective-permute-start | bytes 1622024 | tf_op jit(solution)/shard_map/ppermute | solution.py:728
  385.6 44.9 %collective-permute-start.14 = (f32[8,3328]{1,0:T(8,128)S(1)}, f32[8,3328]{1,0:T(8,128)S(1)}, u32[]{:S(2)}, u32[]{:S(2)}) collective-permute-start(f32[8,3328]{1,0:T(8,128)S(1)} %add.261), channel_id=1, source_target_pairs={{0,2},{1,3},{2,0},{3,1},{4,6},{5,7},{6,4},{7,5},{8,10},{9,11},{10,... | collective-permute-start | bytes 319496 | tf_op jit(solution)/shard_map/ppermute | solution.py:728
  386.7 17.8 %collective-permute-start.25 = (bf16[2,96,1408]{2,1,0:T(8,128)(2,1)S(1)}, bf16[2,96,1408]{2,1,0:T(8,128)(2,1)S(1)}, u32[]{:S(2)}, u32[]{:S(2)}) collective-permute-start(bf16[2,96,1408]{2,1,0:T(8,128)(2,1)S(1)} %dynamic-slice_bitcast_fusion.2), channel_id=1, source_target_pairs={{0,1},{1,0},{2,3},{3,2},{4,5},{5,4},{6,7},{7,6},{8,9},{9,8},{10,11... | collective-permute-start | bytes 1622024 | tf_op jit(solution)/shard_map/ppermute | solution.py:728
  402.7 8.7 %collective-permute-start.28 = (bf16[96,1408]{1,0:T(8,128)(2,1)S(1)}, bf16[96,1408]{1,0:T(8,128)(2,1)S(1)}, u32[]{:S(2)}, u32[]{:S(2)}) collective-permute-start(bf16[96,1408]{1,0:T(8,128)(2,1)S(1)} %dynamic-slice_bitcast_fusion.3), channel_id=1, source_target_pairs={{0,1},{1,0},{2,3},{3,2},{4,5},{5,4},{6,7},{7,6},{8,9},{9,8},{10,11... | collective-permute-start | bytes 811016 | tf_op jit(solution)/shard_map/ppermute | solution.py:728
  404.7 11.9 %collective-permute-start.26 = (bf16[96,1408]{1,0:T(8,128)(2,1)S(1)}, bf16[96,1408]{1,0:T(8,128)(2,1)S(1)}, u32[]{:S(2)}, u32[]{:S(2)}) collective-permute-start(bf16[96,1408]{1,0:T(8,128)(2,1)S(1)} %dynamic-slice_bitcast_fusion.4), channel_id=1, source_target_pairs={{0,2},{1,3},{2,0},{3,1},{4,6},{5,7},{6,4},{7,5},{8,10},{9,11},{10,... | collective-permute-start | bytes 811016 | tf_op jit(solution)/shard_map/ppermute | solution.py:728
  416.7 44.4 %collective-permute-start.29 = (bf16[192,1408]{1,0:T(8,128)(2,1)S(1)}, bf16[192,1408]{1,0:T(8,128)(2,1)S(1)}, u32[]{:S(2)}, u32[]{:S(2)}) collective-permute-start(bf16[192,1408]{1,0:T(8,128)(2,1)S(1)} %pad_maximum_fusion.3), channel_id=1, source_target_pairs={{0,8},{8,0},{16,24},{24,16},{1,9},{9,1},{17,25},{25,17},{2,10},{10... | collective-permute-start | bytes 1622024 | tf_op jit(solution)/shard_map/ppermute | solution.py:728
  417.6 70.5 %collective-permute-start.21 = (bf16[192,2048]{1,0:T(8,128)(2,1)}, bf16[192,2048]{1,0:T(8,128)(2,1)}, u32[]{:S(2)}, u32[]{:S(2)}) collective-permute-start(bf16[192,2048]{1,0:T(8,128)(2,1)} %reduce-scatter.6.cloned.1.call-done), channel_id=1, source_target_pairs={{0,8},{8,0},{16,24},{24,16},{1,9},{9,1},{17,25},{25,17},{2,10},{10... | collective-permute-start | bytes 2359304 | tf_op jit(solution)/shard_map/ppermute | solution.py:728
  430.5 25.8 %collective-permute-start.15 = (f32[8,3328]{1,0:T(8,128)S(1)}, f32[8,3328]{1,0:T(8,128)S(1)}, u32[]{:S(2)}, u32[]{:S(2)}) collective-permute-start(f32[8,3328]{1,0:T(8,128)S(1)} %add.262), channel_id=1, source_target_pairs={{0,8},{8,0},{16,24},{24,16},{1,9},{9,1},{17,25},{25,17},{2,10},{10... | collective-permute-start | bytes 319496 | tf_op jit(solution)/shard_map/ppermute | solution.py:728
  431.3 60.9 %collective-permute-start.17 = (bf16[192,3072]{1,0:T(8,128)(2,1)}, bf16[192,3072]{1,0:T(8,128)(2,1)}, u32[]{:S(2)}, u32[]{:S(2)}) collective-permute-start(bf16[192,3072]{1,0:T(8,128)(2,1)} %reduce-scatter.4.cloned.1.call-done), channel_id=1, source_target_pairs={{0,8},{8,0},{16,24},{24,16},{1,9},{9,1},{17,25},{25,17},{2,10},{10... | collective-permute-start | bytes 3538952 | tf_op jit(solution)/shard_map/ppermute | solution.py:728
  457.0 174.2 %collective-permute-start.16 = (f32[8,3328]{1,0:T(8,128)}, f32[8,3328]{1,0:T(8,128)}, u32[]{:S(2)}, u32[]{:S(2)}) collective-permute-start(f32[8,3328]{1,0:T(8,128)} %add.263), channel_id=1, source_target_pairs={{0,16},{8,24},{16,0},{24,8},{1,17},{9,25},{17,1},{25,9},{2,18},{10... | collective-permute-start | bytes 319496 | tf_op jit(solution)/shard_map/ppermute | solution.py:728
  461.2 33.3 %collective-permute-start.30 = (bf16[192,1408]{1,0:T(8,128)(2,1)S(1)}, bf16[192,1408]{1,0:T(8,128)(2,1)S(1)}, u32[]{:S(2)}, u32[]{:S(2)}) collective-permute-start(bf16[192,1408]{1,0:T(8,128)(2,1)S(1)} %add_convert_fusion.13), channel_id=1, source_target_pairs={{0,16},{8,24},{16,0},{24,8},{1,17},{9,25},{17,1},{25,9},{2,18},{10... | collective-permute-start | bytes 1622024 | tf_op jit(solution)/shard_map/ppermute | solution.py:728
  487.6 49.5 %collective-permute-start.32 = (bf16[768,768]{1,0:T(8,128)(2,1)}, bf16[768,768]{1,0:T(8,128)(2,1)S(1)}, u32[]{:S(2)}, u32[]{:S(2)}) collective-permute-start(bf16[768,768]{1,0:T(8,128)(2,1)} %reduce-scatter.8.cloned.1.call-done), channel_id=1, source_target_pairs={{0,8},{8,0},{16,24},{24,16},{1,9},{9,1},{17,25},{25,17},{2,10},{10... | collective-permute-start | bytes 3538952 | tf_op jit(solution)/shard_map/ppermute | solution.py:728
  489.8 50.8 %collective-permute-start.22 = (bf16[192,2048]{1,0:T(8,128)(2,1)S(1)}, bf16[192,2048]{1,0:T(8,128)(2,1)S(1)}, u32[]{:S(2)}, u32[]{:S(2)}) collective-permute-start(bf16[192,2048]{1,0:T(8,128)(2,1)S(1)} %add_convert_fusion.11), channel_id=1, source_target_pairs={{0,16},{8,24},{16,0},{24,8},{1,17},{9,25},{17,1},{25,9},{2,18},{10... | collective-permute-start | bytes 2359304 | tf_op jit(solution)/shard_map/ppermute | solution.py:728
  493.9 108.9 %collective-permute-start.18 = (bf16[192,3072]{1,0:T(8,128)(2,1)S(1)}, bf16[192,3072]{1,0:T(8,128)(2,1)S(1)}, u32[]{:S(2)}, u32[]{:S(2)}) collective-permute-start(bf16[192,3072]{1,0:T(8,128)(2,1)S(1)} %add_convert_fusion.9), channel_id=1, source_target_pairs={{0,16},{8,24},{16,0},{24,8},{1,17},{9,25},{17,1},{25,9},{2,18},{10... | collective-permute-start | bytes 3538952 | tf_op jit(solution)/shard_map/ppermute | solution.py:728
  494.6 108.6 %copy-start.18 = (bf16[192,1408]{1,0:T(8,128)(2,1)}, bf16[192,1408]{1,0:T(8,128)(2,1)S(1)}, u32[]{:S(2)}) copy-start(bf16[192,1408]{1,0:T(8,128)(2,1)S(1)} %add_convert_fusion.12.refs_4_) | copy-start | bytes 1622020
  494.6 140.6 %collective-permute-start.31 = (bf16[192,1408]{1,0:T(8,128)(2,1)S(1)}, bf16[192,1408]{1,0:T(8,128)(2,1)S(1)}, u32[]{:S(2)}, u32[]{:S(2)}) collective-permute-start(bf16[192,1408]{1,0:T(8,128)(2,1)S(1)} %add_convert_fusion.12.refs_4_), channel_id=1, source_target_pairs={{0,4},{4,0},{1,5},{5,1},{2,6},{6,2},{3,7},{7,3},{8,12},{12,8},{9,1... | collective-permute-start | bytes 1622024 | tf_op jit(solution)/shard_map/ppermute | solution.py:724
  537.3 89.4 %collective-permute-start.33 = (bf16[768,768]{1,0:T(8,128)(2,1)S(1)}, bf16[768,768]{1,0:T(8,128)(2,1)S(1)}, u32[]{:S(2)}, u32[]{:S(2)}) collective-permute-start(bf16[768,768]{1,0:T(8,128)(2,1)S(1)} %add_convert_fusion.7), channel_id=1, source_target_pairs={{0,16},{8,24},{16,0},{24,8},{1,17},{9,25},{17,1},{25,9},{2,18},{10... | collective-permute-start | bytes 3538952 | tf_op jit(solution)/shard_map/ppermute | solution.py:728
  540.6 87.4 %copy-start.10 = (f32[512,1536]{1,0:T(8,128)S(1)}, f32[512,1536]{1,0:T(8,128)}, u32[]{:S(2)}) copy-start(f32[512,1536]{1,0:T(8,128)} %get-tuple-element.151) | copy-start | bytes 9437188
  540.9 87.1 %copy-start.9 = (bf16[192,2048]{1,0:T(8,128)(2,1)}, bf16[192,2048]{1,0:T(8,128)(2,1)S(1)}, u32[]{:S(2)}) copy-start(bf16[192,2048]{1,0:T(8,128)(2,1)S(1)} %add_convert_fusion.10.refs_2_) | copy-start | bytes 2359300
  540.9 87.1 %copy-start.1 = (f32[512,1536]{1,0:T(8,128)S(1)}, f32[512,1536]{1,0:T(8,128)}, u32[]{:S(2)}) copy-start(f32[512,1536]{1,0:T(8,128)} %join_cols.2) | copy-start | bytes 9437188
  540.9 87.1 %copy-start.3 = (bf16[512,1536]{1,0:T(8,128)(2,1)S(1)}, bf16[512,1536]{1,0:T(8,128)(2,1)}, u32[]{:S(2)}) copy-start(bf16[512,1536]{1,0:T(8,128)(2,1)} %param.23) | copy-start | bytes 4718596
  540.9 87.1 %copy-start.36 = (f32[512]{0:T(512)S(1)}, f32[512]{0:T(512)}, u32[]{:S(2)}) copy-start(f32[512]{0:T(512)} %copy-done.34) | copy-start | bytes 6148
  540.9 94.3 %collective-permute-start.23 = (bf16[192,2048]{1,0:T(8,128)(2,1)S(1)}, bf16[192,2048]{1,0:T(8,128)(2,1)S(1)}, u32[]{:S(2)}, u32[]{:S(2)}) collective-permute-start(bf16[192,2048]{1,0:T(8,128)(2,1)S(1)} %add_convert_fusion.10.refs_2_), channel_id=1, source_target_pairs={{0,4},{4,0},{1,5},{5,1},{2,6},{6,2},{3,7},{7,3},{8,12},{12,8},{9,1... | collective-permute-start | bytes 2359304 | tf_op jit(solution)/shard_map/ppermute | solution.py:724
  603.3 33.6 %collective-permute-start.19 = (bf16[192,3072]{1,0:T(8,128)(2,1)S(1)}, bf16[192,3072]{1,0:T(8,128)(2,1)}, u32[]{:S(2)}, u32[]{:S(2)}) collective-permute-start(bf16[192,3072]{1,0:T(8,128)(2,1)S(1)} %add_convert_fusion.8.refs_0_), channel_id=1, source_target_pairs={{0,4},{4,0},{1,5},{5,1},{2,6},{6,2},{3,7},{7,3},{8,12},{12,8},{9,1... | collective-permute-start | bytes 3538952 | tf_op jit(solution)/shard_map/ppermute | solution.py:724
  628.0 29.5 %collective-permute-start.34 = (bf16[768,768]{1,0:T(8,128)(2,1)}, bf16[768,768]{1,0:T(8,128)(2,1)}, u32[]{:S(2)}, u32[]{:S(2)}) collective-permute-start(bf16[768,768]{1,0:T(8,128)(2,1)} %add_convert_fusion.6.mine), channel_id=1, source_target_pairs={{0,4},{4,0},{1,5},{5,1},{2,6},{6,2},{3,7},{7,3},{8,12},{12,8},{9,1... | collective-permute-start | bytes 3538952 | tf_op jit(solution)/shard_map/ppermute | solution.py:724
  (53 other events, 411.4 us)
Sparse Core Ops, SparseCore 0:
  17.9 84.9 all-gather.4
  104.7 57.5 all-gather.6
  309.4 43.9 reduce-scatter.5
  356.8 70.2 reduce-scatter.3
  430.5 57.0 reduce-scatter.7
